TPU v7x, 32 devices: a whole 2x2x4 slice. The times are simulated.
32 devices in a mesh: dp: 8 (over z, y), query: 4 (over x, core).
Axes of the slice: x: 2, y: 2, z: 4, core: 2. Of those that a mesh axis runs over, the one named last changes fastest.
Arguments:
- activations: bfloat16 [4096, 8192], P('dp', 'query'), may hold values from -6 to 6
- grads: bfloat16 [4096, 14336], P('dp', 'query'), may hold values from -6 to 6
- v_factors: bfloat16 [8192, 4096], P('query', 'dp'), may hold values from -0.0625 to 0.0625
- u_factors: bfloat16 [14336, 4096], P('query', 'dp'), may hold values from -0.001953125 to 0.001953125
- candidates: int32 [256, 2], P('dp'), may hold values from 0 to 7, all different within a row; in each aligned block of 32 rows (0 to 31, 32 to 63, ...) at most 16 rows name the same one
Outputs:
- scores: float32 [256, 2, 16], P('dp', None, 'query')
Inputs may be any that keep to these rules, and one draw needn't show every extreme that they name: `candidates`: each row names 2 different query blocks. Among the 32 rows of one index of dp, no query block is named more than 16 times.
All inputs are finite; a program needn't handle non-finite values.
Results may differ from a plain program's by a relative error of at most 0.0003.
Values may be sent and summed in bfloat16 or wider, within the bound.
No kernel may reach another device: no remote copies, remote signals or barrier semaphores. Data moves between devices by JAX's collectives and lax.ppermute only.
A program may use at most 128 MiB of HBM per device.

v0:
```python
import jax
import jax.numpy as jnp
from jax import lax
from jax.sharding import PartitionSpec as P

R = 32


def local_scores(received, v_factors, u_factors, reducer):
    recv_act, recv_grad = received
    peer_total, item_count, token_count, width_act = recv_act.shape
    row_total = peer_total * item_count * token_count
    flat_act = recv_act.reshape(row_total, width_act)
    flat_grad = recv_grad.reshape(row_total, recv_grad.shape[3])

    def partial_term(first_row, row_count):
        proj_act = lax.dot_general(
            v_factors, flat_act, (((0,), (1,)), ((), ())), preferred_element_type=jnp.float32
        )
        proj_grad = lax.dot_general(
            u_factors, flat_grad, (((0,), (1,)), ((), ())), preferred_element_type=jnp.float32
        )
        return jnp.stack([proj_act, proj_grad], axis=1)

    reduced = reducer(partial_term)
    products = reduced[:, 0] * reduced[:, 1]
    local_queries = products.shape[0] // R
    summed = jnp.sum(
        products.reshape(local_queries, R, peer_total, item_count, token_count), axis=(1, 4)
    )
    return jnp.transpose(summed, (1, 2, 0))


def per_device(activations, grads, v_factors, u_factors, candidates):
    peer_total = lax.axis_size("dp")
    blocks = candidates.shape[0]
    pick_count = candidates.shape[1]
    token_count = activations.shape[0] // blocks
    capacity = 2 * blocks * pick_count // peer_total
    width_act = activations.shape[1]
    width_grad = grads.shape[1]
    column_total = v_factors.shape[1]
    local_rows = column_total // lax.axis_size("query")
    entry_total = blocks * pick_count
    slot_total = peer_total * capacity
    target = candidates.reshape(entry_total)
    onehot = (target[:, None] == jnp.arange(peer_total, dtype=jnp.int32)[None, :]).astype(jnp.int32)
    earlier = jnp.cumsum(onehot, axis=0) - onehot
    slot_index = jnp.sum(earlier * onehot, axis=1)
    position = target * capacity + slot_index
    matches = (position[None, :] == jnp.arange(slot_total, dtype=jnp.int32)[:, None]).astype(
        jnp.int32
    )
    owner_block = jnp.arange(entry_total, dtype=jnp.int32) // pick_count
    source = jnp.sum(matches * owner_block[None, :], axis=1)
    filled = jnp.sum(matches, axis=1) > 0
    act_blocks = activations.reshape(blocks, token_count, width_act)
    grad_blocks = grads.reshape(blocks, token_count, width_grad)
    send_act = jnp.where(
        filled[:, None, None],
        jnp.take(act_blocks, source, axis=0),
        jnp.zeros((), activations.dtype),
    )
    send_grad = jnp.where(
        filled[:, None, None], jnp.take(grad_blocks, source, axis=0), jnp.zeros((), grads.dtype)
    )
    send_act = send_act.reshape(peer_total, capacity, token_count, width_act)
    send_grad = send_grad.reshape(peer_total, capacity, token_count, width_grad)
    scored = local_scores(
        (
            lax.all_to_all(send_act, "dp", split_axis=0, concat_axis=0, tiled=True),
            lax.all_to_all(send_grad, "dp", split_axis=0, concat_axis=0, tiled=True),
        ),
        v_factors,
        u_factors,
        lambda partial_term: lax.psum_scatter(
            partial_term(jnp.int32(0), local_rows * lax.axis_size("query")),
            "query",
            scatter_dimension=0,
            tiled=True,
        ),
    )
    returned = lax.all_to_all(scored, "dp", split_axis=0, concat_axis=0, tiled=True)
    flattened = returned.reshape(slot_total, returned.shape[2])
    picked = jnp.take(flattened, position, axis=0)
    return picked.reshape(blocks, pick_count, returned.shape[2])


def solution(mesh):
    placed = (P("dp", "query"), P("dp", "query"), P("query", "dp"), P("query", "dp"), P("dp", None))
    return jax.shard_map(
        per_device, mesh=mesh, in_specs=placed, out_specs=P("dp", None, "query"), check_vma=False
    )
```

profile of v0, /device:TPU:0, one launch (start us, length us, event | category | flops | bytes accessed | tf_op | source)
XLA Modules:
  0.0 650.7 jit_solution(13791531584243853808)
XLA Ops:
  6.5 0.9 copy.31
  7.7 0.2 select_reduce_fusion.1
  8.2 6.5 gather_fusion
  14.7 7.4 %select_select_fusion.1 = bf16[8,16,16,2048]{3,2,1,0:T(8,128)(2,1)} fusion(bf16[8,16,16,2048]{3,2,1,0:T(8,128)(2,1)} %bitcast.36, pred[8,16]{1,0:T(8,128)(4,1)S(1)} %compare_and_fusion, pred[8,16]{1,0:T(8,128)(4,1)S(1)} %gt.19), kind=kLoop, calls=%fused_computation.5 | loop fusion | flops 8388608 | bytes 16777472 | tf_op jit(solution)/shard_map/jit(_where)/select_n | solution.py:59
  22.1 7.3 %all-to-all-start = ((bf16[8,16,16,2048]{3,2,1,0:T(8,128)(2,1)}), bf16[8,16,16,2048]{3,2,1,0:T(8,128)(2,1)}, u32[]{:S(2)}, u32[]{:S(2)}) async-start(bf16[8,16,16,2048]{3,2,1,0:T(8,128)(2,1)} %select_select_fusion.1), calls=%async_computation | async-start | bytes 16777216 | tf_op jit(solution)/shard_map/all_to_all | solution.py:71
  29.4 11.1 %gather_fusion.1 = bf16[128,16,3584]{2,1,0:T(8,128)(2,1)} fusion(bf16[32,16,3584]{2,1,0:T(8,128)(2,1)} %bitcast.35, s32[1024]{0:T(1024)S(1)} %pad_clamp_fusion.1), kind=kCustom, calls=%fused_computation.1 | custom fusion | bytes 29360640 | tf_op jit(solution)/shard_map/jit(_take)/gather | solution.py:65
  40.5 11.1 %select_select_fusion = bf16[8,16,16,3584]{3,2,1,0:T(8,128)(2,1)} fusion(bf16[8,16,16,3584]{3,2,1,0:T(8,128)(2,1)} %bitcast.34, pred[8,16]{1,0:T(8,128)(4,1)S(1)} %compare_and_fusion, pred[8,16]{1,0:T(8,128)(4,1)S(1)} %gt.19), kind=kLoop, calls=%fused_computation.3 | loop fusion | flops 14680064 | bytes 29360384 | tf_op jit(solution)/shard_map/jit(_where)/select_n | solution.py:64
  51.6 160.9 %all-to-all-done = bf16[8,16,16,2048]{3,2,1,0:T(8,128)(2,1)} async-done(((bf16[8,16,16,2048]{3,2,1,0:T(8,128)(2,1)}), bf16[8,16,16,2048]{3,2,1,0:T(8,128)(2,1)}, u32[]{:S(2)}, u32[]{:S(2)}) %all-to-all-start) | async-done | bytes 8388640 | tf_op jit(solution)/shard_map/all_to_all | solution.py:71
  212.6 5.5 all-to-all-start.1
  218.2 9.6 %convolution_bitcast_fusion.1 = f32[512,1,2048]{0,2,1:T(8,128)} fusion(bf16[2048,2048]{1,0:T(8,128)(2,1)} %bitcast.4, bf16[2048,512]{1,0:T(8,128)(2,1)S(1)} %copy-done.4), kind=kOutput, calls=%fused_computation.7 | convolution fusion | flops 4294967296 | bytes 14680064 | tf_op jit(solution)/shard_map/dot_general | solution.py:17
  227.7 307.5 %all-to-all-done.1 = bf16[8,16,16,3584]{3,2,1,0:T(8,128)(2,1)} async-done(((bf16[8,16,16,3584]{3,2,1,0:T(8,128)(2,1)}), bf16[8,16,16,3584]{3,2,1,0:T(8,128)(2,1)}, u32[]{:S(2)}, u32[]{:S(2)}) %all-to-all-start.1) | async-done | bytes 14680096 | tf_op jit(solution)/shard_map/all_to_all | solution.py:72
  535.2 11.9 %convolution_bitcast_fusion = f32[512,1,2048]{0,2,1:T(8,128)S(1)} fusion(bf16[2048,3584]{1,0:T(8,128)(2,1)} %bitcast.9, bf16[3584,512]{1,0:T(8,128)(2,1)} %param.8), kind=kOutput, calls=%fused_computation.6 | convolution fusion | flops 7516192768 | bytes 22544384 | tf_op jit(solution)/shard_map/dot_general | solution.py:20
  547.1 4.2 pad_maximum_fusion
  551.4 0.5 copy-done.3
  552.2 69.5 %reduce-scatter.2.cloned.1.call-done = f32[128,2,2048]{0,2,1:T(8,128)} async-done(((f32[512,2,2048]{0,2,1:T(8,128)}), f32[128,2,2048]{0,2,1:T(8,128)}) %reduce-scatter.2.cloned.1.call-update) | async-done | bytes 2097168 | tf_op jit(solution)/shard_map/reduce_scatter | solution.py:76
  621.7 1.6 slice_multiply_fusion
  623.4 3.2 mul.57
  626.5 3.1 reduce_sum.50
  629.6 0.7 copy.33
  630.3 5.5 all-to-all-start.2
  635.9 6.6 %all-to-all-done.2 = f32[8,16,4]{1,2,0:T(4,128)S(1)} async-done(((f32[8,16,4]{1,2,0:T(4,128)}), f32[8,16,4]{1,2,0:T(4,128)S(1)}, u32[]{:S(2)}, u32[]{:S(2)}) %all-to-all-start.2) | async-done | bytes 2080 | tf_op jit(solution)/shard_map/all_to_all | solution.py:83
  642.4 0.1 copy.34
  642.5 0.6 gather_fusion.2
  643.2 0.6 broadcast_select_fusion
  (31 shorter events, 1.1 us)
Async XLA Ops:
  6.5 1.7 copy-start
  22.1 190.5 %all-to-all-start = ((bf16[8,16,16,2048]{3,2,1,0:T(8,128)(2,1)}), bf16[8,16,16,2048]{3,2,1,0:T(8,128)(2,1)}, u32[]{:S(2)}, u32[]{:S(2)}) async-start(bf16[8,16,16,2048]{3,2,1,0:T(8,128)(2,1)} %select_select_fusion.1), calls=%async_computation | async-start | bytes 16777216 | tf_op jit(solution)/shard_map/all_to_all | solution.py:71
  51.6 166.5 %copy-start.4 = (bf16[2048,512]{1,0:T(8,128)(2,1)S(1)}, bf16[2048,512]{1,0:T(8,128)(2,1)}, u32[]{:S(2)}) copy-start(bf16[2048,512]{1,0:T(8,128)(2,1)} %param.7) | copy-start | bytes 6291460
  212.6 322.6 %all-to-all-start.1 = ((bf16[8,16,16,3584]{3,2,1,0:T(8,128)(2,1)}), bf16[8,16,16,3584]{3,2,1,0:T(8,128)(2,1)}, u32[]{:S(2)}, u32[]{:S(2)}) async-start(bf16[8,16,16,3584]{3,2,1,0:T(8,128)(2,1)} %select_select_fusion), calls=%async_computation.1 | async-start | bytes 29360128 | tf_op jit(solution)/shard_map/all_to_all | solution.py:72
  218.1 403.6 %reduce-scatter.2.cloned.1.call-start = ((), (), s32[]{:S(2)}) async-start(), calls=%async_computation.4 | async-start | bytes 10485760 | tf_op jit(solution)/shard_map/reduce_scatter | solution.py:76
  535.2 11.9 %copy-start.2 = (f32[512,1,2048]{0,2,1:T(8,128)S(1)}, f32[512,1,2048]{0,2,1:T(8,128)}, u32[]{:S(2)}) copy-start(f32[512,1,2048]{0,2,1:T(8,128)} %convolution_bitcast_fusion.1) | copy-start | bytes 12582916
  551.3 0.7 copy-start.3
  551.3 92.5 %copy-start.1 = (bf16[512,2048]{1,0:T(8,128)(2,1)S(1)}, bf16[512,2048]{1,0:T(8,128)(2,1)}, u32[]{:S(2)}) copy-start(bf16[512,2048]{1,0:T(8,128)(2,1)} %param.5) | copy-start | bytes 6291460
  630.3 12.1 %all-to-all-start.2 = ((f32[8,16,4]{1,2,0:T(4,128)}), f32[8,16,4]{1,2,0:T(4,128)S(1)}, u32[]{:S(2)}, u32[]{:S(2)}) async-start(f32[8,16,4]{1,2,0:T(4,128)} %copy.33), calls=%async_computation.3 | async-start | bytes 32768 | tf_op jit(solution)/shard_map/all_to_all | solution.py:83
Sparse Core Ops, SparseCore 0:
  551.4 70.2 reduce-scatter.1
where the time goes:
time: 651 us
  waiting for transfers between devices  544 us (84%)
  other arithmetic  28.5 us (4%)
  local copies, waits for them, and re-layouts  24.4 us (4%)
  matrix products  21.4 us (3%)
  starting transfers between devices  18.4 us (3%)
  between operations  13.5 us (2%)
    all_to_all x1, waiting for transfers between devices, per_device(): lax.all_to_all(send_grad, 'dp', split_axis=0, concat_axis=0, tiled=True)  307 us
    all_to_all x1, waiting for transfers between devices, per_device(): lax.all_to_all(send_act, 'dp', split_axis=0, concat_axis=0, tiled=True)  161 us
    reduce_scatter x1, waiting for transfers between devices, per_device(): lax.psum_scatter(partial_term(jnp.int32(0), local_rows * lax.axis_size('q...  69.5 us
  transfers between devices with their start and end apart: 4, of which 4 were waited for; matrix products, arithmetic and copies ran while one was open for 5% of the time, Pallas kernels for 0%

commit v1 on v0

--- a/solution.py
+++ b/solution.py
@@ -1,9 +1,13 @@
 import jax
 import jax.numpy as jnp
 from jax import lax
+from jax.experimental import pallas as pl
+from jax.experimental.pallas import tpu as pltpu
 from jax.sharding import PartitionSpec as P
 
 R = 32
+TOKENS_PER_BLOCK = 16
+VMEM_BYTES = 64 * 2**20
 
 
 def local_scores(received, v_factors, u_factors, reducer):
@@ -31,7 +35,7 @@
     return jnp.transpose(summed, (1, 2, 0))
 
 
-def per_device(activations, grads, v_factors, u_factors, candidates):
+def exchange_plan(activations, grads, v_factors, u_factors, candidates):
     peer_total = lax.axis_size("dp")
     blocks = candidates.shape[0]
     pick_count = candidates.shape[1]
@@ -86,8 +90,203 @@
     return picked.reshape(blocks, pick_count, returned.shape[2])
 
 
+def swap_pairs(total, mask):
+    return [(index, index ^ mask) for index in range(total)]
+
+
+def projections(units, sources, factors, order, core, after=()):
+    count = len(units)
+    capacity = order.shape[1]
+    width, columns = factors[0].shape
+    token_count = TOKENS_PER_BLOCK
+    rows = capacity * token_count
+    quarter = columns // 4
+
+    def body(order_ref, core_ref, *refs):
+        source_refs = refs[: len(sources)]
+        factor_refs = refs[len(sources) : len(sources) + len(factors)]
+        middle = core_ref[1] == 1
+        keep_ref, send_ref, token_buffer, factor_buffer, token_done, factor_done = refs[-6:]
+
+        def factor_copy(which):
+            return pltpu.make_async_copy(
+                factor_refs[which], factor_buffer.at[which], factor_done.at[which]
+            )
+
+        started = set()
+        for unit, (source, factor, first) in enumerate(units):
+
+            def gather(origin, unit=unit, first=first):
+                for slot in range(capacity):
+                    block = order_ref[first, slot]
+                    pltpu.make_async_copy(
+                        origin.at[pl.ds(block * token_count, token_count)],
+                        token_buffer.at[unit, pl.ds(slot * token_count, token_count)],
+                        token_done.at[unit],
+                    ).start()
+
+            if source == 0:
+                gather(source_refs[0])
+            else:
+                pl.when(middle)(lambda: gather(source_refs[1]))
+                pl.when(jnp.logical_not(middle))(lambda: gather(source_refs[2]))
+            if factor not in started:
+                started.add(factor)
+                factor_copy(factor).start()
+        waited = set()
+        for unit, (source, factor, first) in enumerate(units):
+            pltpu.make_async_copy(
+                source_refs[0].at[pl.ds(0, rows)], token_buffer.at[unit], token_done.at[unit]
+            ).wait()
+            if factor not in waited:
+                waited.add(factor)
+                factor_copy(factor).wait()
+            product = jnp.dot(
+                token_buffer[unit], factor_buffer[factor], preferred_element_type=jnp.float32
+            )
+            span = pl.ds(unit * rows, rows)
+            parts = [product[:, place * quarter : (place + 1) * quarter] for place in range(4)]
+            first_core = core_ref[0] == 0
+            for side in range(2):
+                keep_ref[side, span] = jnp.where(first_core, parts[2 * side], parts[2 * side + 1])
+                send_ref[side, span] = jnp.where(first_core, parts[2 * side + 1], parts[2 * side])
+
+    anywhere = pl.BlockSpec(memory_space=pltpu.HBM)
+    scalars = pl.BlockSpec(memory_space=pltpu.SMEM)
+    result = jax.ShapeDtypeStruct((2, count * rows, quarter), jnp.float32)
+    return pl.pallas_call(
+        body,
+        out_shape=(result, result),
+        in_specs=[scalars, scalars] + [anywhere] * (len(sources) + len(factors) + len(after)),
+        scratch_shapes=[
+            pltpu.VMEM((count, rows, width), sources[0].dtype),
+            pltpu.VMEM((len(factors), width, columns), factors[0].dtype),
+            pltpu.SemaphoreType.DMA((count,)),
+            pltpu.SemaphoreType.DMA((len(factors),)),
+        ],
+        compiler_params=pltpu.CompilerParams(vmem_limit_bytes=VMEM_BYTES),
+    )(order, core, *sources, *factors, *after)
+
+
+def block_scores(acts, gradients, side, positions):
+    rows, quarter = acts[2].shape
+    slots = rows // TOKENS_PER_BLOCK
+    queries = quarter // R
+    entries = positions[0].shape[0]
+    outputs = len(positions)
+
+    def body(side_ref, *refs):
+        keep_a, came_a, far_a, keep_g, came_g, far_g = (ref[...].reshape(rows, quarter) for ref in refs[:6])
+        products = (keep_a + came_a + far_a) * (keep_g + came_g + far_g)
+        per_slot = jnp.sum(products.reshape(slots, TOKENS_PER_BLOCK, quarter), axis=1)
+        lane = lax.broadcasted_iota(jnp.int32, (quarter, queries), 0)
+        query = lax.broadcasted_iota(jnp.int32, (quarter, queries), 1)
+        groups = jnp.where(lane // R == query, 1.0, 0.0).astype(jnp.float32)
+        sums = jnp.dot(
+            per_slot, groups, precision=lax.Precision.HIGHEST, preferred_element_type=jnp.float32
+        )
+        for position_ref, out_ref in zip(refs[6 : 6 + outputs], refs[6 + outputs :]):
+            slot = lax.broadcasted_iota(jnp.int32, (entries, slots), 1)
+            chosen = jnp.where(position_ref[...] == slot, 1.0, 0.0).astype(jnp.float32)
+            out_ref[...] = jnp.dot(
+                chosen, sums, precision=lax.Precision.HIGHEST, preferred_element_type=jnp.float32
+            )
+
+    half = pl.BlockSpec((1, rows, quarter), lambda step, side_ref: (side_ref[0], 0, 0))
+    whole = pl.BlockSpec((rows, quarter), lambda step, side_ref: (0, 0))
+    placed = pl.BlockSpec((entries, 1), lambda step, side_ref: (0, 0))
+    given = pl.BlockSpec((entries, queries), lambda step, side_ref: (0, 0))
+    return pl.pallas_call(
+        body,
+        out_shape=(jax.ShapeDtypeStruct((entries, queries), jnp.float32),) * outputs,
+        grid_spec=pltpu.PrefetchScalarGridSpec(
+            num_scalar_prefetch=1,
+            grid=(1,),
+            in_specs=[half, half, whole] * 2 + [placed] * outputs,
+            out_specs=(given,) * outputs,
+        ),
+    )(side, *acts, *gradients, *positions)
+
+
+def slots_of(named, me, capacity):
+    blocks, pick_count = named.shape
+    entries = blocks * pick_count
+    relative = (named ^ me).reshape(entries)
+    onehot = (relative[:, None] == jnp.arange(4, dtype=jnp.int32)[None, :]).astype(jnp.int32)
+    earlier = jnp.cumsum(onehot, axis=0) - onehot
+    position = relative * capacity + jnp.sum(earlier * onehot, axis=1)
+    position = jnp.where(relative < 4, position, -1)
+    matches = position[None, :] == jnp.arange(4 * capacity, dtype=jnp.int32)[:, None]
+    owner = jnp.arange(entries, dtype=jnp.int32) // pick_count
+    order = jnp.sum(jnp.where(matches, owner[None, :], 0), axis=1)
+    return order.reshape(4, capacity), position.reshape(entries, 1)
+
+
+def mirror_plan(activations, grads, v_factors, u_factors, candidates):
+    me = lax.axis_index("dp")
+    place = lax.axis_index("query")
+    side = (place // 2).reshape(1)
+    blocks, pick_count = candidates.shape
+    capacity = 2 * blocks * pick_count // 8
+    across_z = swap_pairs(8, 2)
+    across_y = swap_pairs(8, 1)
+    mirror = swap_pairs(8, 6)
+    inner = mirror[2:6]
+    outer = mirror[:2] + mirror[6:]
+    is_inner = jnp.logical_and(me >= 2, me < 6).astype(jnp.int32)
+    core = jnp.stack([place % 2, is_inner])
+
+    def swap(array, pairs):
+        return lax.ppermute(array, "dp", pairs)
+
+    mirrored = swap(candidates, mirror)
+    u_y = swap(u_factors, across_y)
+    u_z = swap(u_factors, across_z)
+    v_y = swap(v_factors, across_y)
+    v_z = swap(v_factors, across_z)
+    g_in = swap(grads, inner)
+    a_in = swap(activations, inner)
+    g_out = swap(grads, outer)
+    a_out = swap(activations, outer)
+    u_d = swap(u_z, across_y)
+    v_d = swap(v_z, across_y)
+
+    near_order, near_position = slots_of(candidates, me, capacity)
+    far_order, far_position = slots_of(mirrored, me, capacity)
+    order = jnp.concatenate([near_order, far_order], axis=0)
+
+    def reduced(halves):
+        keep, send = halves
+        came = lax.ppermute(send, "query", swap_pairs(4, 1))
+        other = 1 - side[0]
+        onward = lax.dynamic_index_in_dim(keep, other, 0, False) + lax.dynamic_index_in_dim(
+            came, other, 0, False
+        )
+        return keep, came, lax.ppermute(onward, "query", swap_pairs(4, 2))
+
+    first = [(0, 0, 0), (0, 1, 1), (0, 2, 2)]
+    last = [(0, 3, 3), (1, 0, 4), (1, 1, 5), (1, 2, 6), (1, 3, 7)]
+    u_first = projections(first, [grads], [u_factors, u_y, u_z], order, core)
+    v_first = projections(first, [activations], [v_factors, v_y, v_z], order, core, u_first[:1])
+    (near_first,) = block_scores(reduced(v_first), reduced(u_first), side, (near_position,))
+    u_last = projections(last, [grads, g_in, g_out], [u_factors, u_y, u_z, u_d], order, core, (near_first,))
+    v_last = projections(last, [activations, a_in, a_out], [v_factors, v_y, v_z, v_d], order, core, u_last[:1])
+    near_slot = jnp.where(near_position >= 3 * capacity, near_position - 3 * capacity, -1)
+    far_slot = jnp.where(far_position >= 0, far_position + capacity, -1)
+    near_last, far = block_scores(reduced(v_last), reduced(u_last), side, (near_slot, far_slot))
+    total = near_first + near_last + swap(far, mirror)
+    return total.reshape(blocks, pick_count, total.shape[1])
+
+
 def solution(mesh):
     placed = (P("dp", "query"), P("dp", "query"), P("query", "dp"), P("query", "dp"), P("dp", None))
+    grid = mesh.shape["dp"] == 8 and mesh.shape["query"] == 4
+
+    def step(*operands):
+        if not grid:
+            return exchange_plan(*operands)
+        return mirror_plan(*operands)
+
     return jax.shard_map(
-        per_device, mesh=mesh, in_specs=placed, out_specs=P("dp", None, "query"), check_vma=False
-    )
+        step, mesh=mesh, in_specs=placed, out_specs=P("dp", None, "query"), check_vma=False
+    )

time: 651 us -> 348 us (0.53)
  the two profiles are of different devices: /device:TPU:0 before, /device:TPU:8 now
where the time goes in v1:
time: 348 us; the launch traced here: 347 us
  waiting for transfers between devices  263 us (76%)
  Pallas kernels  45.9 us (13%)
  starting transfers between devices  25.7 us (7%)
  other arithmetic  10 us (3%)
    ppermute x12, waiting for transfers between devices, swap(): return lax.ppermute(array, 'dp', pairs)  223 us
    pallas_call x4, Pallas kernels, projections(): pl.pallas_call(body, out_shape=(result, result), in_specs=[scalars, scala...  39.9 us
    ppermute x4, waiting for transfers between devices, reduced(): return (keep, came, lax.ppermute(onward, 'query', swap_pairs(4, 2)))  37.2 us
    ppermute x12, starting transfers between devices, swap(): return lax.ppermute(array, 'dp', pairs)  19.7 us
  transfers between devices with their start and end apart: 20, of which 12 were waited for; matrix products, arithmetic and copies ran while one was open for 3% of the time, Pallas kernels for 12%

profile of v1, /device:TPU:8, one launch (start us, length us, event | category | flops | bytes accessed | tf_op | source)
XLA Modules:
  0.0 347.4 jit_solution(2328137433088520274)
XLA Ops:
  0.0 2.0 collective-permute-start.3
  2.0 4.6 %collective-permute-start.12 = (bf16[512,3584]{1,0:T(8,128)(2,1)}, bf16[512,3584]{1,0:T(8,128)(2,1)}, u32[]{:S(2)}, u32[]{:S(2)}) collective-permute-start(bf16[512,3584]{1,0:T(8,128)(2,1)} %refs_0_.6), channel_id=1, source_target_pairs={{8,16},{12,20},{16,8},{20,12},{9,17},{13,21},{17,9},{21,13},{10,18... | collective-permute-start | bytes 11010056 | tf_op jit(solution)/shard_map/ppermute | solution.py:240
  6.7 1.8 collective-permute-start.2
  8.5 77.2 %collective-permute-done = s32[32,2]{0,1:T(2,128)S(1)} collective-permute-done((s32[32,2]{0,1:T(2,128)}, s32[32,2]{0,1:T(2,128)S(1)}, u32[]{:S(2)}, u32[]{:S(2)}) %collective-permute-start) | collective-permute-done | bytes 288 | tf_op jit(solution)/shard_map/ppermute | solution.py:240
  90.5 2.5 collective-permute-start.13
  95.5 9.5 %shard_map.55 = (f32[2,768,128]{2,1,0:T(8,128)}, f32[2,768,128]{2,1,0:T(8,128)}) custom-call(s32[8,16]{1,0:T(8,128)} %pad_add_fusion.order_ref, s32[2]{0:T(128)} %pad_add_fusion.1.core_ref, bf16[512,3584]{1,0:T(8,128)(2,1)} %refs_0_.6, bf16[3584,512]{1,0:T(8,128)(2,1)} %refs_3_.2, bf16[3584,512]{1,0:T(8,128)(2,1)} %collective-permute-done.3.refs_2_.refs_4_, ...), custom_call_target="tpu_custom_call" | custom-call | tf_op jit(solution)/shard_map/pallas_call | solution.py:157
  105.0 22.5 %collective-permute-done.2.refs_3_.refs_5_ = bf16[2048,512]{1,0:T(8,128)(2,1)} collective-permute-done((bf16[2048,512]{1,0:T(8,128)(2,1)}, bf16[2048,512]{1,0:T(8,128)(2,1)}, u32[]{:S(2)}, u32[]{:S(2)}) %collective-permute-start.2) | collective-permute-done | bytes 2097184 | tf_op jit(solution)/shard_map/ppermute | solution.py:240
  127.5 7.0 %collective-permute-done.1.refs_2_.refs_4_ = bf16[2048,512]{1,0:T(8,128)(2,1)} collective-permute-done((bf16[2048,512]{1,0:T(8,128)(2,1)}, bf16[2048,512]{1,0:T(8,128)(2,1)}, u32[]{:S(2)}, u32[]{:S(2)}) %collective-permute-start.1) | collective-permute-done | bytes 2097184 | tf_op jit(solution)/shard_map/ppermute | solution.py:240
  134.5 7.2 %shard_map.56 = (f32[2,768,128]{2,1,0:T(8,128)}, f32[2,768,128]{2,1,0:T(8,128)}) custom-call(s32[8,16]{1,0:T(8,128)} %pad_add_fusion.order_ref, s32[2]{0:T(128)} %pad_add_fusion.1.core_ref, bf16[512,2048]{1,0:T(8,128)(2,1)} %refs_0_.7, bf16[2048,512]{1,0:T(8,128)(2,1)} %refs_3_.3, bf16[2048,512]{1,0:T(8,128)(2,1)} %collective-permute-done.1.refs_2_.refs_4_, ...), custom_call_target="tpu_custom_call" | custom-call | tf_op jit(solution)/shard_map/pallas_call | solution.py:157
  142.4 2.0 collective-permute-done.5.refs_1_
  145.7 1.6 collective-permute-start.6
  149.1 2.0 collective-permute-start.10
  151.1 6.6 %collective-permute-done.6.refs_2_ = f32[768,128]{1,0:T(8,128)S(1)} collective-permute-done((f32[768,128]{1,0:T(8,128)S(1)}, f32[768,128]{1,0:T(8,128)S(1)}, u32[]{:S(2)}, u32[]{:S(2)}) %collective-permute-start.6) | collective-permute-done | bytes 393248 | tf_op jit(solution)/shard_map/ppermute | solution.py:265
  157.7 3.8 %collective-permute-start.9 = (bf16[512,2048]{1,0:T(8,128)(2,1)}, bf16[512,2048]{1,0:T(8,128)(2,1)}, u32[]{:S(2)}, u32[]{:S(2)}) collective-permute-start(bf16[512,2048]{1,0:T(8,128)(2,1)} %refs_0_.7), channel_id=1, source_target_pairs={{8,16},{12,20},{16,8},{20,12},{9,17},{13,21},{17,9},{21,13},{10,18... | collective-permute-start | bytes 6291464 | tf_op jit(solution)/shard_map/ppermute | solution.py:240
  161.5 3.8 %collective-permute-done.8.refs_5_ = f32[768,128]{1,0:T(8,128)S(1)} collective-permute-done((f32[768,128]{1,0:T(8,128)S(1)}, f32[768,128]{1,0:T(8,128)S(1)}, u32[]{:S(2)}, u32[]{:S(2)}) %collective-permute-start.8) | collective-permute-done | bytes 393248 | tf_op jit(solution)/shard_map/ppermute | solution.py:265
  166.9 2.7 shard_map.57.refs_7_
  169.6 43.6 %collective-permute-done.14.refs_6_ = bf16[3584,512]{1,0:T(8,128)(2,1)} collective-permute-done((bf16[3584,512]{1,0:T(8,128)(2,1)}, bf16[3584,512]{1,0:T(8,128)(2,1)}, u32[]{:S(2)}, u32[]{:S(2)}) %collective-permute-start.14) | collective-permute-done | bytes 3670048 | tf_op jit(solution)/shard_map/ppermute | solution.py:240
  213.2 13.4 %shard_map.58 = (f32[2,1280,128]{2,1,0:T(8,128)}, f32[2,1280,128]{2,1,0:T(8,128)}) custom-call(s32[8,16]{1,0:T(8,128)} %pad_add_fusion.order_ref, s32[2]{0:T(128)} %pad_add_fusion.1.core_ref, bf16[512,3584]{1,0:T(8,128)(2,1)} %refs_0_.6, bf16[512,3584]{1,0:T(8,128)(2,1)} %collective-permute-done.12.refs_1_, ...), custom_call_target="tpu_custom_call" | custom-call | tf_op jit(solution)/shard_map/pallas_call | solution.py:157
  226.7 69.2 %collective-permute-done.9.refs_1_ = bf16[512,2048]{1,0:T(8,128)(2,1)} collective-permute-done((bf16[512,2048]{1,0:T(8,128)(2,1)}, bf16[512,2048]{1,0:T(8,128)(2,1)}, u32[]{:S(2)}, u32[]{:S(2)}) %collective-permute-start.9) | collective-permute-done | bytes 2097184 | tf_op jit(solution)/shard_map/ppermute | solution.py:240
  295.9 9.7 %shard_map.59 = (f32[2,1280,128]{2,1,0:T(8,128)}, f32[2,1280,128]{2,1,0:T(8,128)}) custom-call(s32[8,16]{1,0:T(8,128)} %pad_add_fusion.order_ref, s32[2]{0:T(128)} %pad_add_fusion.1.core_ref, bf16[512,2048]{1,0:T(8,128)(2,1)} %refs_0_.7, bf16[512,2048]{1,0:T(8,128)(2,1)} %collective-permute-done.9.refs_1_, ...), custom_call_target="tpu_custom_call" | custom-call | tf_op jit(solution)/shard_map/pallas_call | solution.py:157
  311.7 13.2 %collective-permute-done.18.refs_5_ = f32[1280,128]{1,0:T(8,128)S(1)} collective-permute-done((f32[1280,128]{1,0:T(8,128)S(1)}, f32[1280,128]{1,0:T(8,128)S(1)}, u32[]{:S(2)}, u32[]{:S(2)}) %collective-permute-start.18) | collective-permute-done | bytes 655392 | tf_op jit(solution)/shard_map/ppermute | solution.py:265
  324.9 13.6 %collective-permute-done.16.refs_2_ = f32[1280,128]{1,0:T(8,128)} collective-permute-done((f32[1280,128]{1,0:T(8,128)S(1)}, f32[1280,128]{1,0:T(8,128)}, u32[]{:S(2)}, u32[]{:S(2)}) %collective-permute-start.16) | collective-permute-done | bytes 655392 | tf_op jit(solution)/shard_map/ppermute | solution.py:265
  338.5 3.4 shard_map.60
  342.3 3.7 %collective-permute-done.19 = f32[64,4]{1,0:T(8,128)S(1)} collective-permute-done((f32[64,4]{1,0:T(8,128)}, f32[64,4]{1,0:T(8,128)S(1)}, u32[]{:S(2)}, u32[]{:S(2)}) %collective-permute-start.19) | collective-permute-done | bytes 1056 | tf_op jit(solution)/shard_map/ppermute | solution.py:240
  (97 shorter events, 20.6 us)
Async XLA Ops:
  0.0 90.5 %collective-permute-start.4 = (bf16[3584,512]{1,0:T(8,128)(2,1)}, bf16[3584,512]{1,0:T(8,128)(2,1)}, u32[]{:S(2)}, u32[]{:S(2)}) collective-permute-start(bf16[3584,512]{1,0:T(8,128)(2,1)} %refs_3_.2), channel_id=1, source_target_pairs={{0,8},{4,12},{8,0},{12,4},{16,24},{20,28},{24,16},{28,20},{1,9},{5... | collective-permute-start | bytes 11010056 | tf_op jit(solution)/shard_map/ppermute | solution.py:240
  0.0 93.1 %collective-permute-start.3 = (bf16[3584,512]{1,0:T(8,128)(2,1)}, bf16[3584,512]{1,0:T(8,128)(2,1)}, u32[]{:S(2)}, u32[]{:S(2)}) collective-permute-start(bf16[3584,512]{1,0:T(8,128)(2,1)} %refs_3_.2), channel_id=1, source_target_pairs={{0,4},{4,0},{8,12},{12,8},{16,20},{20,16},{24,28},{28,24},{1,5},{5... | collective-permute-start | bytes 11010056 | tf_op jit(solution)/shard_map/ppermute | solution.py:240
  2.0 147.1 %collective-permute-start.12 = (bf16[512,3584]{1,0:T(8,128)(2,1)}, bf16[512,3584]{1,0:T(8,128)(2,1)}, u32[]{:S(2)}, u32[]{:S(2)}) collective-permute-start(bf16[512,3584]{1,0:T(8,128)(2,1)} %refs_0_.6), channel_id=1, source_target_pairs={{8,16},{12,20},{16,8},{20,12},{9,17},{13,21},{17,9},{21,13},{10,18... | collective-permute-start | bytes 11010056 | tf_op jit(solution)/shard_map/ppermute | solution.py:240
  6.6 79.1 %collective-permute-start = (s32[32,2]{0,1:T(2,128)}, s32[32,2]{0,1:T(2,128)S(1)}, u32[]{:S(2)}, u32[]{:S(2)}) collective-permute-start(s32[32,2]{0,1:T(2,128)} %param.9), channel_id=1, source_target_pairs={{0,24},{4,28},{8,16},{12,20},{16,8},{20,12},{24,0},{28,4},{1,25},{... | collective-permute-start | bytes 776 | tf_op jit(solution)/shard_map/ppermute | solution.py:240
  6.7 120.8 %collective-permute-start.2 = (bf16[2048,512]{1,0:T(8,128)(2,1)}, bf16[2048,512]{1,0:T(8,128)(2,1)}, u32[]{:S(2)}, u32[]{:S(2)}) collective-permute-start(bf16[2048,512]{1,0:T(8,128)(2,1)} %refs_3_.3), channel_id=1, source_target_pairs={{0,8},{4,12},{8,0},{12,4},{16,24},{20,28},{24,16},{28,20},{1,9},{5... | collective-permute-start | bytes 6291464 | tf_op jit(solution)/shard_map/ppermute | solution.py:240
  85.7 48.8 %collective-permute-start.1 = (bf16[2048,512]{1,0:T(8,128)(2,1)}, bf16[2048,512]{1,0:T(8,128)(2,1)}, u32[]{:S(2)}, u32[]{:S(2)}) collective-permute-start(bf16[2048,512]{1,0:T(8,128)(2,1)} %refs_3_.3), channel_id=1, source_target_pairs={{0,4},{4,0},{8,12},{12,8},{16,20},{20,16},{24,28},{28,24},{1,5},{5... | collective-permute-start | bytes 6291464 | tf_op jit(solution)/shard_map/ppermute | solution.py:240
  90.5 79.0 %collective-permute-start.13 = (bf16[512,3584]{1,0:T(8,128)(2,1)}, bf16[512,3584]{1,0:T(8,128)(2,1)}, u32[]{:S(2)}, u32[]{:S(2)}) collective-permute-start(bf16[512,3584]{1,0:T(8,128)(2,1)} %refs_0_.6), channel_id=1, source_target_pairs={{0,24},{4,28},{24,0},{28,4},{1,25},{5,29},{25,1},{29,5},{2,26},{6,... | collective-permute-start | bytes 11010056 | tf_op jit(solution)/shard_map/ppermute | solution.py:240
  93.1 120.1 %collective-permute-start.14 = (bf16[3584,512]{1,0:T(8,128)(2,1)}, bf16[3584,512]{1,0:T(8,128)(2,1)}, u32[]{:S(2)}, u32[]{:S(2)}) collective-permute-start(bf16[3584,512]{1,0:T(8,128)(2,1)} %collective-permute-done.4.refs_3_.refs_5_), channel_id=1, source_target_pairs={{0,4},{4,0},{8,12},{12,8},{16,20},{20,16},{24,28},{28,24},{1,5},{5... | collective-permute-start | bytes 11010056 | tf_op jit(solution)/shard_map/ppermute | solution.py:240
  141.8 24.0 %copy-start.17 = (s32[64]{0:T(128)S(1)}, s32[64]{0:T(128)}, u32[]{:S(2)}) copy-start(s32[64]{0:T(128)} %copy-done.16) | copy-start | bytes 772
  141.8 24.1 %copy-start.15 = (s32[32,2]{0,1:T(2,128)S(1)}, s32[32,2]{0,1:T(2,128)}, u32[]{:S(2)}) copy-start(s32[32,2]{0,1:T(2,128)} %copy-done.14) | copy-start | bytes 772
  141.8 24.3 %copy-start.13 = (s32[32,2]{0,1:T(2,128)S(1)}, s32[32,2]{0,1:T(2,128)}, u32[]{:S(2)}) copy-start(s32[32,2]{0,1:T(2,128)} %get-tuple-element.31) | copy-start | bytes 772
  141.8 2.6 collective-permute-start.5
  141.9 5.3 %collective-permute-start.7 = (f32[2,768,128]{2,1,0:T(8,128)}, f32[2,768,128]{2,1,0:T(8,128)S(1)}, u32[]{:S(2)}, u32[]{:S(2)}) collective-permute-start(f32[2,768,128]{2,1,0:T(8,128)} %get-tuple-element.18), channel_id=1, source_target_pairs={{0,1},{1,0},{2,3},{3,2},{4,5},{5,4},{6,7},{7,6},{8,9},{9,8},{10,11... | collective-permute-start | bytes 2359304 | tf_op jit(solution)/shard_map/ppermute | solution.py:260
  145.7 12.1 %collective-permute-start.6 = (f32[768,128]{1,0:T(8,128)S(1)}, f32[768,128]{1,0:T(8,128)S(1)}, u32[]{:S(2)}, u32[]{:S(2)}) collective-permute-start(f32[768,128]{1,0:T(8,128)S(1)} %add_bitcast_fusion.3), channel_id=1, source_target_pairs={{0,2},{1,3},{2,0},{3,1},{4,6},{5,7},{6,4},{7,5},{8,10},{9,11},{10,... | collective-permute-start | bytes 1179656 | tf_op jit(solution)/shard_map/ppermute | solution.py:265
  148.5 16.8 %collective-permute-start.8 = (f32[768,128]{1,0:T(8,128)S(1)}, f32[768,128]{1,0:T(8,128)S(1)}, u32[]{:S(2)}, u32[]{:S(2)}) collective-permute-start(f32[768,128]{1,0:T(8,128)S(1)} %add_bitcast_fusion.2), channel_id=1, source_target_pairs={{0,2},{1,3},{2,0},{3,1},{4,6},{5,7},{6,4},{7,5},{8,10},{9,11},{10,... | collective-permute-start | bytes 1179656 | tf_op jit(solution)/shard_map/ppermute | solution.py:265
  149.1 77.6 %collective-permute-start.10 = (bf16[512,2048]{1,0:T(8,128)(2,1)}, bf16[512,2048]{1,0:T(8,128)(2,1)}, u32[]{:S(2)}, u32[]{:S(2)}) collective-permute-start(bf16[512,2048]{1,0:T(8,128)(2,1)} %refs_0_.7), channel_id=1, source_target_pairs={{0,24},{4,28},{24,0},{28,4},{1,25},{5,29},{25,1},{29,5},{2,26},{6,... | collective-permute-start | bytes 6291464 | tf_op jit(solution)/shard_map/ppermute | solution.py:240
  157.7 138.2 %collective-permute-start.9 = (bf16[512,2048]{1,0:T(8,128)(2,1)}, bf16[512,2048]{1,0:T(8,128)(2,1)}, u32[]{:S(2)}, u32[]{:S(2)}) collective-permute-start(bf16[512,2048]{1,0:T(8,128)(2,1)} %refs_0_.7), channel_id=1, source_target_pairs={{8,16},{12,20},{16,8},{20,12},{9,17},{13,21},{17,9},{21,13},{10,18... | collective-permute-start | bytes 6291464 | tf_op jit(solution)/shard_map/ppermute | solution.py:240
  165.3 130.6 %collective-permute-start.11 = (bf16[2048,512]{1,0:T(8,128)(2,1)}, bf16[2048,512]{1,0:T(8,128)(2,1)}, u32[]{:S(2)}, u32[]{:S(2)}) collective-permute-start(bf16[2048,512]{1,0:T(8,128)(2,1)} %collective-permute-done.2.refs_3_.refs_5_), channel_id=1, source_target_pairs={{0,4},{4,0},{8,12},{12,8},{16,20},{20,16},{24,28},{28,24},{1,5},{5... | collective-permute-start | bytes 6291464 | tf_op jit(solution)/shard_map/ppermute | solution.py:240
  226.6 79.1 %collective-permute-start.17 = (f32[2,1280,128]{2,1,0:T(8,128)}, f32[2,1280,128]{2,1,0:T(8,128)}, u32[]{:S(2)}, u32[]{:S(2)}) collective-permute-start(f32[2,1280,128]{2,1,0:T(8,128)} %get-tuple-element.22), channel_id=1, source_target_pairs={{0,1},{1,0},{2,3},{3,2},{4,5},{5,4},{6,7},{7,6},{8,9},{9,8},{10,11... | collective-permute-start | bytes 3932168 | tf_op jit(solution)/shard_map/ppermute | solution.py:260
  305.7 3.3 collective-permute-start.15
  307.2 17.7 %collective-permute-start.18 = (f32[1280,128]{1,0:T(8,128)S(1)}, f32[1280,128]{1,0:T(8,128)S(1)}, u32[]{:S(2)}, u32[]{:S(2)}) collective-permute-start(f32[1280,128]{1,0:T(8,128)S(1)} %add_bitcast_fusion), channel_id=1, source_target_pairs={{0,2},{1,3},{2,0},{3,1},{4,6},{5,7},{6,4},{7,5},{8,10},{9,11},{10,... | collective-permute-start | bytes 1966088 | tf_op jit(solution)/shard_map/ppermute | solution.py:265
  309.0 29.5 %copy-start.1 = (f32[2,1280,128]{2,1,0:T(8,128)}, f32[2,1280,128]{2,1,0:T(8,128)S(1)}, u32[]{:S(2)}) copy-start(f32[2,1280,128]{2,1,0:T(8,128)S(1)} %collective-permute-done.15.refs_1_) | copy-start | bytes 3932164
  309.1 29.4 %collective-permute-start.16 = (f32[1280,128]{1,0:T(8,128)S(1)}, f32[1280,128]{1,0:T(8,128)}, u32[]{:S(2)}, u32[]{:S(2)}) collective-permute-start(f32[1280,128]{1,0:T(8,128)S(1)} %add_bitcast_fusion.1), channel_id=1, source_target_pairs={{0,2},{1,3},{2,0},{3,1},{4,6},{5,7},{6,4},{7,5},{8,10},{9,11},{10,... | collective-permute-start | bytes 1966088 | tf_op jit(solution)/shard_map/ppermute | solution.py:265
  341.8 4.1 %collective-permute-start.19 = (f32[64,4]{1,0:T(8,128)}, f32[64,4]{1,0:T(8,128)S(1)}, u32[]{:S(2)}, u32[]{:S(2)}) collective-permute-start(f32[64,4]{1,0:T(8,128)} %get-tuple-element.24), channel_id=1, source_target_pairs={{0,24},{4,28},{8,16},{12,20},{16,8},{20,12},{24,0},{28,4},{1,25},{... | collective-permute-start | bytes 3080 | tf_op jit(solution)/shard_map/ppermute | solution.py:240
  (14 other events, 98.8 us)

commit v2 on v0

--- a/solution.py
+++ b/solution.py
@@ -1,9 +1,13 @@
 import jax
 import jax.numpy as jnp
 from jax import lax
+from jax.experimental import pallas as pl
+from jax.experimental.pallas import tpu as pltpu
 from jax.sharding import PartitionSpec as P
 
 R = 32
+TOKENS_PER_BLOCK = 16
+VMEM_BYTES = 64 * 2**20
 
 
 def local_scores(received, v_factors, u_factors, reducer):
@@ -31,7 +35,7 @@
     return jnp.transpose(summed, (1, 2, 0))
 
 
-def per_device(activations, grads, v_factors, u_factors, candidates):
+def exchange_plan(activations, grads, v_factors, u_factors, candidates):
     peer_total = lax.axis_size("dp")
     blocks = candidates.shape[0]
     pick_count = candidates.shape[1]
@@ -86,8 +90,346 @@
     return picked.reshape(blocks, pick_count, returned.shape[2])
 
 
+def swap_pairs(total, mask):
+    return [(index, index ^ mask) for index in range(total)]
+
+
+def grouped_products(units, sources, factors, order, flags, totals=None, bases=(), after=()):
+    count = len(units)
+    capacity = order.shape[1]
+    width, columns = factors[0].shape
+    token_count = TOKENS_PER_BLOCK
+    rows = capacity * token_count
+    part = rows // 2
+    quarter = columns // 4
+    queries = quarter // R
+    dense = any(factor is None for _, factor, _ in units)
+    first_total, own_total, partner_total, positions = totals if totals else (0, None, None, ())
+    kinds = len(positions)
+    held = len(sources) + len(factors) + len(after)
+    added = [base for base in bases if base is not None]
+
+    def body(order_ref, flags_ref, *refs):
+        source_refs = refs[: len(sources)]
+        factor_refs = refs[len(sources) : len(sources) + len(factors)]
+        given = refs[held:]
+        token_buffer, factor_buffer, product_buffer, sum_buffer, token_done, factor_done = refs[-6:]
+        step = pl.program_id(0)
+        first_core = flags_ref[0] == 0
+        middle = flags_ref[1] == 1
+
+        def factor_copy(which):
+            return pltpu.make_async_copy(
+                factor_refs[which], factor_buffer.at[which], factor_done.at[which]
+            )
+
+        def token_copy(origin, origin_row, unit, row, length):
+            return pltpu.make_async_copy(
+                origin.at[pl.ds(origin_row, length)],
+                token_buffer.at[unit, pl.ds(row, length)],
+                token_done.at[unit],
+            )
+
+        def fetch(unit):
+            source, factor, first = units[unit]
+
+            def gather(origin):
+                for slot in range(capacity):
+                    block = order_ref[first, slot]
+                    token_copy(origin, block * token_count, unit, slot * token_count, token_count).start()
+
+            if factor is None:
+                inner, outer = source_refs[1], source_refs[-1]
+                whole, end = sources[1].shape[0], sources[-1].shape[0]
+                pl.when(middle)(lambda: token_copy(inner, whole - part, unit, 0, part).start())
+                pl.when(jnp.logical_not(middle))(
+                    lambda: token_copy(outer, end - part, unit, 0, part).start()
+                )
+            elif source == 0:
+                gather(source_refs[0])
+            else:
+                pl.when(middle)(lambda: gather(source_refs[1]))
+                pl.when(jnp.logical_not(middle))(lambda: gather(source_refs[2]))
+
+        def give(unit, row, height, values):
+            pieces = [values[:, place * quarter : (place + 1) * quarter] for place in range(4)]
+            for side in range(2):
+                even, odd = pieces[2 * side], pieces[2 * side + 1]
+                span = pl.ds(row, height)
+                if totals is None:
+                    keep_ref, send_ref = given[:2]
+                    keep_ref[side, span] = jnp.where(first_core, even, odd)
+                    send_ref[side, span] = jnp.where(first_core, odd, even)
+                else:
+                    own, partner = given[0][side, span], given[1][side, span]
+                    slots = pl.ds(unit * capacity + row // token_count, height // token_count)
+                    for core, piece in enumerate((even, odd)):
+                        total = jnp.where(first_core == (core == 0), own, partner)
+                        product = (piece * total).reshape(height // token_count, token_count, quarter)
+                        sum_buffer[2 * side + core, slots] = jnp.sum(product, axis=1)
+
+        def times(unit, height, which):
+            return jnp.dot(
+                token_buffer[unit, :height], factor_buffer[which], preferred_element_type=jnp.float32
+            )
+
+        def compute(unit, fresh):
+            _, factor, first = units[unit]
+            height = part if factor is None else rows
+            token_copy(source_refs[0], 0, unit, 0, height).wait()
+            if factor is not None:
+                if factor in fresh:
+                    factor_copy(factor).wait()
+                give(unit, 0, rows, times(unit, rows, factor))
+                return
+            for which in range(len(factors)):
+                if which in fresh:
+                    factor_copy(which).wait()
+                product_buffer[which] = times(unit, part, which)
+            for entry in range(capacity):
+                which = order_ref[first, entry]
+                row = entry // 2 * token_count
+                product_buffer[len(factors) + entry // 8, entry % 8 * token_count : (entry % 8 + 1) * token_count] = (
+                    product_buffer[which, row : row + token_count]
+                )
+            for half in range(2):
+                give(unit, half * part, part, product_buffer[len(factors) + half])
+
+        def finish():
+            place = flags_ref[2]
+            lane = lax.broadcasted_iota(jnp.int32, (4 * queries, quarter), 1)
+            query = lax.broadcasted_iota(jnp.int32, (4 * queries, quarter), 0)
+            sums = jnp.zeros((4 * queries, count * capacity), jnp.float32)
+            for block in range(4):
+                groups = jnp.where(lane // R + queries * block == query, 1.0, 0.0).astype(jnp.float32)
+                sums = sums + lax.dot_general(
+                    groups,
+                    sum_buffer[block],
+                    (((1,), (1,)), ((), ())),
+                    precision=lax.Precision.HIGHEST,
+                    preferred_element_type=jnp.float32,
+                )
+            position_refs = given[2 : 2 + kinds]
+            base_refs = list(given[2 + kinds : 2 + kinds + len(added)])
+            out_refs = given[2 + kinds + len(added) : 2 + kinds + len(added) + kinds]
+            for kind in range(kinds):
+                wanted = position_refs[kind][...]
+                slot = lax.broadcasted_iota(jnp.int32, (count * capacity, wanted.shape[1]), 0)
+                values = jnp.dot(
+                    sums,
+                    jnp.where(wanted == slot, 1.0, 0.0).astype(jnp.float32),
+                    precision=lax.Precision.HIGHEST,
+                    preferred_element_type=jnp.float32,
+                )
+                parts = [values[queries * block : queries * (block + 1)] for block in range(4)]
+                base_ref = base_refs.pop(0) if bases[kind] is not None else None
+                for offset in range(4):
+                    mine = parts[offset]
+                    for index in range(1, 4):
+                        mine = jnp.where(place == index, parts[index ^ offset], mine)
+                    if base_ref is not None:
+                        mine = mine + base_ref[offset]
+                    out_refs[kind][offset] = mine
+
+        @pl.when(step == 0)
+        def _():
+            started = set()
+            for unit, (source, factor, first) in enumerate(units):
+                fetch(unit)
+                for which in range(len(factors)) if factor is None else (factor,):
+                    if which not in started:
+                        started.add(which)
+                        factor_copy(which).start()
+
+        seen = set()
+        for unit, (source, factor, first) in enumerate(units):
+            used = set(range(len(factors))) if factor is None else {factor}
+            pl.when(step == unit)(lambda unit=unit, fresh=used - seen: compute(unit, fresh))
+            seen |= used
+        if totals is not None:
+            pl.when(step == count - 1)(finish)
+
+    anywhere = pl.BlockSpec(memory_space=pltpu.HBM)
+    scalars = pl.BlockSpec(memory_space=pltpu.SMEM)
+
+    def whole(shape):
+        return pl.BlockSpec(shape, lambda step: (0,) * len(shape))
+
+    in_specs = [scalars, scalars] + [anywhere] * held
+    operands = [order, flags, *sources, *factors, *after]
+    if totals is None:
+        result = jax.ShapeDtypeStruct((2, count * rows, quarter), jnp.float32)
+        out_shape = (result, result)
+        out_specs = (pl.BlockSpec((2, rows, quarter), lambda step: (0, step, 0)),) * 2
+    else:
+        shape = (4, queries, positions[0].shape[1])
+        total_spec = pl.BlockSpec((2, rows, quarter), lambda step: (0, step + first_total, 0))
+        in_specs += [total_spec] * 2 + [whole(positions[0].shape)] * kinds + [whole(shape)] * len(added)
+        operands += [own_total, partner_total, *positions, *added]
+        out_shape = (jax.ShapeDtypeStruct(shape, jnp.float32),) * kinds
+        out_specs = (whole(shape),) * kinds
+    return pl.pallas_call(
+        body,
+        grid=(count,),
+        out_shape=out_shape,
+        in_specs=in_specs,
+        out_specs=out_specs,
+        scratch_shapes=[
+            pltpu.VMEM((count, rows, width), sources[0].dtype),
+            pltpu.VMEM((len(factors), width, columns), factors[0].dtype),
+            pltpu.VMEM((len(factors) + 2 if dense else 1, part, columns), jnp.float32),
+            pltpu.VMEM((4, count * capacity, quarter), jnp.float32),
+            pltpu.SemaphoreType.DMA((count,)),
+            pltpu.SemaphoreType.DMA((len(factors),)),
+        ],
+        compiler_params=pltpu.CompilerParams(vmem_limit_bytes=VMEM_BYTES),
+    )(*operands)
+
+
+def slots_of(relative, pick_count, capacity):
+    entries = relative.shape[0]
+    onehot = (relative[:, None] == jnp.arange(4, dtype=jnp.int32)[None, :]).astype(jnp.int32)
+    earlier = jnp.cumsum(onehot, axis=0) - onehot
+    slot = jnp.sum(earlier * onehot, axis=1)
+    position = jnp.where(relative < 4, relative * capacity + slot, -1)
+    matches = position[None, :] == jnp.arange(4 * capacity, dtype=jnp.int32)[:, None]
+    owner = jnp.arange(entries, dtype=jnp.int32) // pick_count
+    order = jnp.sum(jnp.where(matches, owner[None, :], 0), axis=1)
+    return order.reshape(4, capacity), position
+
+
+def mirror_plan(activations, grads, v_factors, u_factors, candidates):
+    me = lax.axis_index("dp")
+    place = lax.axis_index("query")
+    blocks, pick_count = candidates.shape
+    entries = blocks * pick_count
+    capacity = 2 * entries // 8
+    late = capacity // 2
+    early_rows = (blocks - late) * TOKENS_PER_BLOCK
+    across_z = swap_pairs(8, 2)
+    across_y = swap_pairs(8, 1)
+    mirror = swap_pairs(8, 6)
+    inner = mirror[2:6]
+    outer = mirror[:2] + mirror[6:]
+    is_inner = jnp.logical_and(me >= 2, me < 6).astype(jnp.int32)
+    flags = jnp.stack([place % 2, is_inner, place])
+
+    def swap(array, pairs, axis="dp"):
+        return lax.ppermute(array, axis, pairs)
+
+    grads_early, grads_late = grads[:early_rows], grads[early_rows:]
+    acts_early, acts_late = activations[:early_rows], activations[early_rows:]
+    mirrored = swap(candidates, mirror)
+    u_y = swap(u_factors, across_y)
+    u_z = swap(u_factors, across_z)
+    v_y = swap(v_factors, across_y)
+    v_z = swap(v_factors, across_z)
+    g_in = swap(grads, inner)
+    a_in = swap(activations, inner)
+    g_out = swap(grads_early, outer)
+    g_end = swap(grads_late, outer)
+    a_out = swap(acts_early, outer)
+    a_end = swap(acts_late, outer)
+    u_d = swap(u_z, across_y)
+    v_d = swap(v_z, across_y)
+
+    three, four = 3 * capacity, 4 * capacity
+    entry = jnp.arange(entries, dtype=jnp.int32)
+
+    def placed(position, low, high, shift):
+        chosen = jnp.logical_and(position >= low, position < high)
+        return jnp.where(chosen, position + shift, -1).reshape(blocks, pick_count).T.reshape(1, entries)
+
+    def summed(halves):
+        keep, send = halves
+        mine = keep + swap(send, swap_pairs(4, 1), "query")
+        mine = mine + swap(mine, swap_pairs(4, 2), "query")
+        return mine, swap(mine, swap_pairs(4, 1), "query")
+
+    near_order, near_position = slots_of((candidates ^ me).reshape(entries), pick_count, capacity)
+    near_three = placed(near_position, 0, three, 0)
+    near_fourth = placed(near_position, three, four, -three)
+    first = [(0, 0, 0), (0, 1, 1), (0, 2, 2)]
+    slices = (grads_early, grads_late, acts_early, acts_late)
+    u_first = grouped_products(first, [grads], [u_factors, u_y, u_z], near_order, flags, after=slices)
+    g_first = summed(u_first)
+    mirrored, _ = lax.optimization_barrier((mirrored, u_first[0]))
+    far_relative = (mirrored ^ me).reshape(entries)
+    is_late = entry >= entries - 2 * late
+    far_order, far_position = slots_of(jnp.where(is_late, 4, far_relative), pick_count, capacity)
+    end_order = jnp.minimum(far_relative[entries - 2 * late :], 3)
+    order = jnp.concatenate([near_order, far_order, end_order[None]], axis=0)
+    far_three = placed(far_position, 0, three, 0)
+    far_fourth = placed(far_position, three, four, capacity - three)
+    end_position = jnp.where(far_relative < 4, entry - (entries - 2 * late), -1)
+    end_position = placed(end_position, 0, capacity, 0)
+
+    (near,) = grouped_products(
+        first,
+        [activations],
+        [v_factors, v_y, v_z],
+        near_order,
+        flags,
+        totals=(0, *g_first, (near_three,)),
+        bases=(None,),
+    )
+    straight = [(1, 0, 4), (1, 1, 5), (1, 2, 6)]
+    u_far = grouped_products(
+        straight, [grads, g_in, g_out], [u_factors, u_y, u_z], order, flags, after=(near, near_fourth, far_three, far_fourth, end_position)
+    )
+    g_far = summed(u_far)
+    u_diagonal = grouped_products([(0, 0, 3), (1, 0, 7)], [grads, g_in, g_out], [u_d], order, flags, after=u_far[:1])
+    g_diagonal = summed(u_diagonal)
+    ending = [(1, None, 8)]
+    u_end = grouped_products(
+        ending, [grads, g_in, g_end], [u_factors, u_y, u_z, u_d], order, flags, after=u_diagonal[:1]
+    )
+    g_ending = summed(u_end)
+    (far,) = grouped_products(
+        straight,
+        [activations, a_in, a_out],
+        [v_factors, v_y, v_z],
+        order,
+        flags,
+        totals=(0, *g_far, (far_three,)),
+        bases=(None,),
+        after=u_end[:1],
+    )
+    near, far = grouped_products(
+        [(0, 0, 3), (1, 0, 7)],
+        [activations, a_in, a_out],
+        [v_d],
+        order,
+        flags,
+        totals=(0, *g_diagonal, (near_fourth, far_fourth)),
+        bases=(near, far),
+    )
+    (far,) = grouped_products(
+        ending,
+        [activations, a_in, a_end],
+        [v_factors, v_y, v_z, v_d],
+        order,
+        flags,
+        totals=(0, *g_ending, (end_position,)),
+        bases=(far,),
+        after=(near,),
+    )
+    partial = near + swap(far, mirror)
+    total = partial[0]
+    for offset in (1, 2, 3):
+        total = total + swap(partial[offset], swap_pairs(4, offset), "query")
+    return jnp.transpose(total.reshape(total.shape[0], pick_count, blocks), (2, 1, 0))
+
+
 def solution(mesh):
     placed = (P("dp", "query"), P("dp", "query"), P("query", "dp"), P("query", "dp"), P("dp", None))
+    grid = mesh.shape["dp"] == 8 and mesh.shape["query"] == 4
+
+    def step(*operands):
+        if not grid:
+            return exchange_plan(*operands)
+        return mirror_plan(*operands)
+
     return jax.shard_map(
-        per_device, mesh=mesh, in_specs=placed, out_specs=P("dp", None, "query"), check_vma=False
-    )
+        step, mesh=mesh, in_specs=placed, out_specs=P("dp", None, "query"), check_vma=False
+    )

time: 651 us -> 405 us (0.62)
  the two profiles are of different devices: /device:TPU:0 before, /device:TPU:9 now
where the time goes in v2:
time: 405 us; the launch traced here: 404 us
  waiting for transfers between devices  270 us (67%)
  Pallas kernels  64.6 us (16%)
  starting transfers between devices  38 us (9%)
  local copies, waits for them, and re-layouts  17.1 us (4%)
  other arithmetic  14.3 us (4%)
    ppermute x29, waiting for transfers between devices, swap(): return lax.ppermute(array, axis, pairs)  270 us
    pallas_call x8, Pallas kernels, grouped_products(): pl.pallas_call(body, grid=(count,), out_shape=out_shape, in_specs=in_spec...  64.6 us
    ppermute x29, starting transfers between devices, swap(): return lax.ppermute(array, axis, pairs)  38 us
  transfers between devices with their start and end apart: 29, of which 10 were waited for; matrix products, arithmetic and copies ran while one was open for 7% of the time, Pallas kernels for 12%

profile of v2, /device:TPU:9, one launch (start us, length us, event | category | flops | bytes accessed | tf_op | source)
XLA Modules:
  0.0 404.1 jit_solution(9956719362571353279)
XLA Ops:
  1.4 3.6 slice.28.refs_4_
  5.0 2.2 slice.29.refs_5_
  12.5 68.1 %collective-permute-done.2.refs_3_.refs_5_ = bf16[3584,512]{1,0:T(8,128)(2,1)} collective-permute-done((bf16[3584,512]{1,0:T(8,128)(2,1)}, bf16[3584,512]{1,0:T(8,128)(2,1)}, u32[]{:S(2)}, u32[]{:S(2)}) %collective-permute-start.2) | collective-permute-done | bytes 3670048 | tf_op jit(solution)/shard_map/ppermute | solution.py:318
  80.6 9.5 %shard_map.55 = (f32[2,768,128]{2,1,0:T(8,128)}, f32[2,768,128]{2,1,0:T(8,128)}) custom-call(s32[4,16]{1,0:T(4,128)} %reshape.107.order_ref, s32[3]{0:T(128)} %pad_add_fusion.1.flags_ref, bf16[512,3584]{1,0:T(8,128)(2,1)} %refs_0_.12, bf16[3584,512]{1,0:T(8,128)(2,1)} %refs_3_.5, bf16[3584,512]{1,0:T(8,128)(2,1)} %collective-permute-done.1.refs_2_.refs_4_, ...), custom_call_target="tpu_custom_call" | custom-call | tf_op jit(solution)/shard_map/pallas_call | solution.py:271
  91.7 4.7 %collective-permute-start.7 = (bf16[512,3584]{1,0:T(8,128)(2,1)}, bf16[512,3584]{1,0:T(8,128)(2,1)}, u32[]{:S(2)}, u32[]{:S(2)}) collective-permute-start(bf16[512,3584]{1,0:T(8,128)(2,1)} %refs_0_.12), channel_id=1, source_target_pairs={{8,16},{12,20},{16,8},{20,12},{9,17},{13,21},{17,9},{21,13},{10,18... | collective-permute-start | bytes 11010056 | tf_op jit(solution)/shard_map/ppermute | solution.py:318
  100.6 135.4 %collective-permute-done = s32[32,2]{1,0:T(8,128)S(1)} collective-permute-done((s32[32,2]{1,0:T(8,128)}, s32[32,2]{1,0:T(8,128)S(1)}, u32[]{:S(2)}, u32[]{:S(2)}) %collective-permute-start) | collective-permute-done | bytes 288 | tf_op jit(solution)/shard_map/ppermute | solution.py:318
  236.0 2.2 collective-permute-start.8
  247.7 37.6 %collective-permute-done.10.refs_2_.refs_4_ = bf16[2048,512]{1,0:T(8,128)(2,1)} collective-permute-done((bf16[2048,512]{1,0:T(8,128)(2,1)}, bf16[2048,512]{1,0:T(8,128)(2,1)}, u32[]{:S(2)}, u32[]{:S(2)}) %collective-permute-start.10) | collective-permute-done | bytes 2097184 | tf_op jit(solution)/shard_map/ppermute | solution.py:318
  285.2 8.1 %shard_map.56.refs_6_.refs_8_ = f32[4,4,64]{2,1,0:T(4,128)} custom-call(s32[4,16]{1,0:T(4,128)} %reshape.107.order_ref, s32[3]{0:T(128)} %pad_add_fusion.1.flags_ref, bf16[512,2048]{1,0:T(8,128)(2,1)} %refs_0_.15, bf16[2048,512]{1,0:T(8,128)(2,1)} %refs_3_.7, bf16[2048,512]{1,0:T(8,128)(2,1)} %collective-permute-done.10.refs_2_.refs_4_, ...), custom_call_target="tpu_custom_call" | custom-call | tf_op jit(solution)/shard_map/pallas_call | solution.py:271
  293.4 10.3 %shard_map.57 = (f32[2,768,128]{2,1,0:T(8,128)}, f32[2,768,128]{2,1,0:T(8,128)}) custom-call(s32[9,16]{1,0:T(8,128)} %pad_add_fusion.order_ref, s32[3]{0:T(128)} %pad_add_fusion.1.flags_ref, bf16[512,3584]{1,0:T(8,128)(2,1)} %refs_0_.12, bf16[512,3584]{1,0:T(8,128)(2,1)} %collective-permute-done.7.refs_1_, bf16[384,3584]{1,0:T(8,128)(2,1)} %collective-permute-done.8.refs_2_, ...), custom_call_target="tpu_custom_call" | custom-call | tf_op jit(solution)/shard_map/pallas_call | solution.py:271
  305.1 7.2 %shard_map.58 = (f32[2,512,128]{2,1,0:T(8,128)}, f32[2,512,128]{2,1,0:T(8,128)}) custom-call(s32[9,16]{1,0:T(8,128)} %pad_add_fusion.order_ref, s32[3]{0:T(128)} %pad_add_fusion.1.flags_ref, bf16[512,3584]{1,0:T(8,128)(2,1)} %refs_0_.12, bf16[512,3584]{1,0:T(8,128)(2,1)} %collective-permute-done.7.refs_1_, bf16[384,3584]{1,0:T(8,128)(2,1)} %collective-permute-done.8.refs_2_, ...), custom_call_target="tpu_custom_call" | custom-call | tf_op jit(solution)/shard_map/pallas_call | solution.py:271
  312.5 2.9 collective-permute-start.3
  319.9 2.4 add.99
  323.4 1.9 add.97
  325.6 8.7 %shard_map.59 = (f32[2,256,128]{2,1,0:T(8,128)}, f32[2,256,128]{2,1,0:T(8,128)}) custom-call(s32[9,16]{1,0:T(8,128)} %pad_add_fusion.order_ref, s32[3]{0:T(128)} %pad_add_fusion.1.flags_ref, bf16[512,3584]{1,0:T(8,128)(2,1)} %refs_0_.12, bf16[512,3584]{1,0:T(8,128)(2,1)} %collective-permute-done.7.refs_1_, ...), custom_call_target="tpu_custom_call" | custom-call | tf_op jit(solution)/shard_map/pallas_call | solution.py:271
  334.3 6.4 %collective-permute-done.19 = f32[2,768,128]{2,1,0:T(8,128)} collective-permute-done((f32[2,768,128]{2,1,0:T(8,128)}, f32[2,768,128]{2,1,0:T(8,128)}, u32[]{:S(2)}, u32[]{:S(2)}) %collective-permute-start.19) | collective-permute-done | bytes 786464 | tf_op jit(solution)/shard_map/ppermute | solution.py:318
  340.6 3.3 collective-permute-start.22
  347.3 4.6 %collective-permute-done.15 = f32[2,512,128]{2,1,0:T(8,128)} collective-permute-done((f32[2,512,128]{2,1,0:T(8,128)}, f32[2,512,128]{2,1,0:T(8,128)}, u32[]{:S(2)}, u32[]{:S(2)}) %collective-permute-start.15) | collective-permute-done | bytes 524320 | tf_op jit(solution)/shard_map/ppermute | solution.py:318
  353.1 2.0 add.98.refs_4_
  355.1 2.1 collective-permute-start.16
  360.2 13.1 %collective-permute-done.3.refs_1_ = bf16[512,2048]{1,0:T(8,128)(2,1)} collective-permute-done((bf16[512,2048]{1,0:T(8,128)(2,1)}, bf16[512,2048]{1,0:T(8,128)(2,1)}, u32[]{:S(2)}, u32[]{:S(2)}) %collective-permute-start.3) | collective-permute-done | bytes 2097184 | tf_op jit(solution)/shard_map/ppermute | solution.py:318
  373.7 8.0 %shard_map.60.refs_9_ = f32[4,4,64]{2,1,0:T(4,128)} custom-call(s32[9,16]{1,0:T(8,128)} %pad_add_fusion.order_ref, s32[3]{0:T(128)} %pad_add_fusion.1.flags_ref, bf16[512,2048]{1,0:T(8,128)(2,1)} %refs_0_.15, bf16[512,2048]{1,0:T(8,128)(2,1)} %collective-permute-done.3.refs_1_, bf16[384,2048]{1,0:T(8,128)(2,1)} %collective-permute-done.4.refs_2_, ...), custom_call_target="tpu_custom_call" | custom-call | tf_op jit(solution)/shard_map/pallas_call | solution.py:271
  381.8 5.8 %shard_map.61 = (f32[4,4,64]{2,1,0:T(4,128)}, f32[4,4,64]{2,1,0:T(4,128)}) custom-call(s32[9,16]{1,0:T(8,128)} %pad_add_fusion.order_ref, s32[3]{0:T(128)} %pad_add_fusion.1.flags_ref, bf16[512,2048]{1,0:T(8,128)(2,1)} %refs_0_.15, bf16[512,2048]{1,0:T(8,128)(2,1)} %collective-permute-done.3.refs_1_, bf16[384,2048]{1,0:T(8,128)(2,1)} %collective-permute-done.4.refs_2_, ...), custom_call_target="tpu_custom_call" | custom-call | tf_op jit(solution)/shard_map/pallas_call | solution.py:271
  387.6 6.9 %shard_map.62 = f32[4,4,64]{2,1,0:T(4,128)} custom-call(s32[9,16]{1,0:T(8,128)} %pad_add_fusion.order_ref, s32[3]{0:T(128)} %pad_add_fusion.1.flags_ref, bf16[512,2048]{1,0:T(8,128)(2,1)} %refs_0_.15, bf16[512,2048]{1,0:T(8,128)(2,1)} %collective-permute-done.3.refs_1_, bf16[128,2048]{1,0:T(8,128)(2,1)} %collective-permute-done.21.refs_2_, ...), custom_call_target="tpu_custom_call" | custom-call | tf_op jit(solution)/shard_map/pallas_call | solution.py:271
  (113 shorter events, 46.9 us)
Async XLA Ops:
  0.0 80.5 %collective-permute-start.2 = (bf16[3584,512]{1,0:T(8,128)(2,1)}, bf16[3584,512]{1,0:T(8,128)(2,1)}, u32[]{:S(2)}, u32[]{:S(2)}) collective-permute-start(bf16[3584,512]{1,0:T(8,128)(2,1)} %refs_3_.5), channel_id=1, source_target_pairs={{0,8},{4,12},{8,0},{12,4},{16,24},{20,28},{24,16},{28,20},{1,9},{5... | collective-permute-start | bytes 11010056 | tf_op jit(solution)/shard_map/ppermute | solution.py:318
  0.0 80.6 %collective-permute-start.1 = (bf16[3584,512]{1,0:T(8,128)(2,1)}, bf16[3584,512]{1,0:T(8,128)(2,1)}, u32[]{:S(2)}, u32[]{:S(2)}) collective-permute-start(bf16[3584,512]{1,0:T(8,128)(2,1)} %refs_3_.5), channel_id=1, source_target_pairs={{0,4},{4,0},{8,12},{12,8},{16,20},{20,16},{24,28},{28,24},{1,5},{5... | collective-permute-start | bytes 11010056 | tf_op jit(solution)/shard_map/ppermute | solution.py:318
  90.1 7.4 %collective-permute-start.11 = (f32[2,768,128]{2,1,0:T(8,128)}, f32[2,768,128]{2,1,0:T(8,128)S(1)}, u32[]{:S(2)}, u32[]{:S(2)}) collective-permute-start(f32[2,768,128]{2,1,0:T(8,128)} %get-tuple-element.18), channel_id=1, source_target_pairs={{0,1},{1,0},{2,3},{3,2},{4,5},{5,4},{6,7},{7,6},{8,9},{9,8},{10,11... | collective-permute-start | bytes 2359304 | tf_op jit(solution)/shard_map/ppermute | solution.py:318
  91.7 201.7 %collective-permute-start.7 = (bf16[512,3584]{1,0:T(8,128)(2,1)}, bf16[512,3584]{1,0:T(8,128)(2,1)}, u32[]{:S(2)}, u32[]{:S(2)}) collective-permute-start(bf16[512,3584]{1,0:T(8,128)(2,1)} %refs_0_.12), channel_id=1, source_target_pairs={{8,16},{12,20},{16,8},{20,12},{9,17},{13,21},{17,9},{21,13},{10,18... | collective-permute-start | bytes 11010056 | tf_op jit(solution)/shard_map/ppermute | solution.py:318
  96.4 208.7 %collective-permute-start.9 = (bf16[3584,512]{1,0:T(8,128)(2,1)}, bf16[3584,512]{1,0:T(8,128)(2,1)}, u32[]{:S(2)}, u32[]{:S(2)}) collective-permute-start(bf16[3584,512]{1,0:T(8,128)(2,1)} %collective-permute-done.2.refs_3_.refs_5_), channel_id=1, source_target_pairs={{0,4},{4,0},{8,12},{12,8},{16,20},{20,16},{24,28},{28,24},{1,5},{5... | collective-permute-start | bytes 11010056 | tf_op jit(solution)/shard_map/ppermute | solution.py:318
  97.5 145.4 %collective-permute-start.5 = (bf16[2048,512]{1,0:T(8,128)(2,1)}, bf16[2048,512]{1,0:T(8,128)(2,1)}, u32[]{:S(2)}, u32[]{:S(2)}) collective-permute-start(bf16[2048,512]{1,0:T(8,128)(2,1)} %refs_3_.7), channel_id=1, source_target_pairs={{0,8},{4,12},{8,0},{12,4},{16,24},{20,28},{24,16},{28,20},{1,9},{5... | collective-permute-start | bytes 6291464 | tf_op jit(solution)/shard_map/ppermute | solution.py:318
  98.7 139.5 %collective-permute-start.12 = (f32[2,768,128]{2,1,0:T(8,128)S(1)}, f32[2,768,128]{2,1,0:T(8,128)S(1)}, u32[]{:S(2)}, u32[]{:S(2)}) collective-permute-start(f32[2,768,128]{2,1,0:T(8,128)S(1)} %add.89), channel_id=1, source_target_pairs={{0,2},{1,3},{2,0},{3,1},{4,6},{5,7},{6,4},{7,5},{8,10},{9,11},{10,... | collective-permute-start | bytes 2359304 | tf_op jit(solution)/shard_map/ppermute | solution.py:318
  100.0 136.1 %collective-permute-start = (s32[32,2]{1,0:T(8,128)}, s32[32,2]{1,0:T(8,128)S(1)}, u32[]{:S(2)}, u32[]{:S(2)}) collective-permute-start(s32[32,2]{1,0:T(8,128)} %copy-done.3), channel_id=1, source_target_pairs={{0,24},{4,28},{8,16},{12,20},{16,8},{20,12},{24,0},{28,4},{1,25},{... | collective-permute-start | bytes 776 | tf_op jit(solution)/shard_map/ppermute | solution.py:318
  236.0 57.3 %collective-permute-start.8 = (bf16[384,3584]{1,0:T(8,128)(2,1)}, bf16[384,3584]{1,0:T(8,128)(2,1)}, u32[]{:S(2)}, u32[]{:S(2)}) collective-permute-start(bf16[384,3584]{1,0:T(8,128)(2,1)} %slice.28.refs_4_), channel_id=1, source_target_pairs={{0,24},{4,28},{24,0},{28,4},{1,25},{5,29},{25,1},{29,5},{2,26},{6,... | collective-permute-start | bytes 8257544 | tf_op jit(solution)/shard_map/ppermute | solution.py:318
  238.2 47.0 %collective-permute-start.10 = (bf16[2048,512]{1,0:T(8,128)(2,1)}, bf16[2048,512]{1,0:T(8,128)(2,1)}, u32[]{:S(2)}, u32[]{:S(2)}) collective-permute-start(bf16[2048,512]{1,0:T(8,128)(2,1)} %refs_3_.7), channel_id=1, source_target_pairs={{0,4},{4,0},{8,12},{12,8},{16,20},{20,16},{24,28},{28,24},{1,5},{5... | collective-permute-start | bytes 6291464 | tf_op jit(solution)/shard_map/ppermute | solution.py:318
  243.8 41.5 %collective-permute-start.13 = (f32[2,768,128]{2,1,0:T(8,128)S(1)}, f32[2,768,128]{2,1,0:T(8,128)}, u32[]{:S(2)}, u32[]{:S(2)}) collective-permute-start(f32[2,768,128]{2,1,0:T(8,128)S(1)} %add.90.refs_4_), channel_id=1, source_target_pairs={{0,1},{1,0},{2,3},{3,2},{4,5},{5,4},{6,7},{7,6},{8,9},{9,8},{10,11... | collective-permute-start | bytes 2359304 | tf_op jit(solution)/shard_map/ppermute | solution.py:318
  303.7 15.1 %collective-permute-start.18 = (f32[2,768,128]{2,1,0:T(8,128)}, f32[2,768,128]{2,1,0:T(8,128)}, u32[]{:S(2)}, u32[]{:S(2)}) collective-permute-start(f32[2,768,128]{2,1,0:T(8,128)} %get-tuple-element.23), channel_id=1, source_target_pairs={{0,1},{1,0},{2,3},{3,2},{4,5},{5,4},{6,7},{7,6},{8,9},{9,8},{10,11... | collective-permute-start | bytes 2359304 | tf_op jit(solution)/shard_map/ppermute | solution.py:318
  312.3 9.9 %collective-permute-start.14 = (f32[2,512,128]{2,1,0:T(8,128)}, f32[2,512,128]{2,1,0:T(8,128)S(1)}, u32[]{:S(2)}, u32[]{:S(2)}) collective-permute-start(f32[2,512,128]{2,1,0:T(8,128)} %get-tuple-element.21), channel_id=1, source_target_pairs={{0,1},{1,0},{2,3},{3,2},{4,5},{5,4},{6,7},{7,6},{8,9},{9,8},{10,11... | collective-permute-start | bytes 1572872 | tf_op jit(solution)/shard_map/ppermute | solution.py:318
  312.5 60.8 %collective-permute-start.3 = (bf16[512,2048]{1,0:T(8,128)(2,1)}, bf16[512,2048]{1,0:T(8,128)(2,1)}, u32[]{:S(2)}, u32[]{:S(2)}) collective-permute-start(bf16[512,2048]{1,0:T(8,128)(2,1)} %refs_0_.15), channel_id=1, source_target_pairs={{8,16},{12,20},{16,8},{20,12},{9,17},{13,21},{17,9},{21,13},{10,18... | collective-permute-start | bytes 6291464 | tf_op jit(solution)/shard_map/ppermute | solution.py:318
  315.3 10.0 %collective-permute-start.17 = (bf16[128,3584]{1,0:T(8,128)(2,1)}, bf16[128,3584]{1,0:T(8,128)(2,1)}, u32[]{:S(2)}, u32[]{:S(2)}) collective-permute-start(bf16[128,3584]{1,0:T(8,128)(2,1)} %slice.29.refs_5_), channel_id=1, source_target_pairs={{0,24},{4,28},{24,0},{28,4},{1,25},{5,29},{25,1},{29,5},{2,26},{6,... | collective-permute-start | bytes 2752520 | tf_op jit(solution)/shard_map/ppermute | solution.py:318
  316.9 38.2 %collective-permute-start.4 = (bf16[384,2048]{1,0:T(8,128)(2,1)}, bf16[384,2048]{1,0:T(8,128)(2,1)}, u32[]{:S(2)}, u32[]{:S(2)}) collective-permute-start(bf16[384,2048]{1,0:T(8,128)(2,1)} %slice.30.refs_6_), channel_id=1, source_target_pairs={{0,24},{4,28},{24,0},{28,4},{1,25},{5,29},{25,1},{29,5},{2,26},{6,... | collective-permute-start | bytes 4718600 | tf_op jit(solution)/shard_map/ppermute | solution.py:318
  318.7 63.0 %collective-permute-start.6 = (bf16[2048,512]{1,0:T(8,128)(2,1)}, bf16[2048,512]{1,0:T(8,128)(2,1)}, u32[]{:S(2)}, u32[]{:S(2)}) collective-permute-start(bf16[2048,512]{1,0:T(8,128)(2,1)} %collective-permute-done.5.refs_3_.refs_5_), channel_id=1, source_target_pairs={{0,4},{4,0},{8,12},{12,8},{16,20},{20,16},{24,28},{28,24},{1,5},{5... | collective-permute-start | bytes 6291464 | tf_op jit(solution)/shard_map/ppermute | solution.py:318
  322.2 18.4 %collective-permute-start.19 = (f32[2,768,128]{2,1,0:T(8,128)}, f32[2,768,128]{2,1,0:T(8,128)}, u32[]{:S(2)}, u32[]{:S(2)}) collective-permute-start(f32[2,768,128]{2,1,0:T(8,128)} %add.99), channel_id=1, source_target_pairs={{0,2},{1,3},{2,0},{3,1},{4,6},{5,7},{6,4},{7,5},{8,10},{9,11},{10,... | collective-permute-start | bytes 2359304 | tf_op jit(solution)/shard_map/ppermute | solution.py:318
  325.3 26.5 %collective-permute-start.15 = (f32[2,512,128]{2,1,0:T(8,128)}, f32[2,512,128]{2,1,0:T(8,128)}, u32[]{:S(2)}, u32[]{:S(2)}) collective-permute-start(f32[2,512,128]{2,1,0:T(8,128)} %add.97), channel_id=1, source_target_pairs={{0,2},{1,3},{2,0},{3,1},{4,6},{5,7},{6,4},{7,5},{8,10},{9,11},{10,... | collective-permute-start | bytes 1572872 | tf_op jit(solution)/shard_map/ppermute | solution.py:318
  346.3 27.4 %collective-permute-start.20 = (f32[2,768,128]{2,1,0:T(8,128)S(1)}, f32[2,768,128]{2,1,0:T(8,128)}, u32[]{:S(2)}, u32[]{:S(2)}) collective-permute-start(f32[2,768,128]{2,1,0:T(8,128)S(1)} %add.100.refs_7_), channel_id=1, source_target_pairs={{0,1},{1,0},{2,3},{3,2},{4,5},{5,4},{6,7},{7,6},{8,9},{9,8},{10,11... | collective-permute-start | bytes 2359304 | tf_op jit(solution)/shard_map/ppermute | solution.py:318
  351.9 6.1 %collective-permute-start.23 = (f32[2,256,128]{2,1,0:T(8,128)S(1)}, f32[2,256,128]{2,1,0:T(8,128)S(1)}, u32[]{:S(2)}, u32[]{:S(2)}) collective-permute-start(f32[2,256,128]{2,1,0:T(8,128)S(1)} %add.101), channel_id=1, source_target_pairs={{0,2},{1,3},{2,0},{3,1},{4,6},{5,7},{6,4},{7,5},{8,10},{9,11},{10,... | collective-permute-start | bytes 786440 | tf_op jit(solution)/shard_map/ppermute | solution.py:318
  355.1 26.6 %collective-permute-start.16 = (f32[2,512,128]{2,1,0:T(8,128)}, f32[2,512,128]{2,1,0:T(8,128)}, u32[]{:S(2)}, u32[]{:S(2)}) collective-permute-start(f32[2,512,128]{2,1,0:T(8,128)} %add.98.refs_4_), channel_id=1, source_target_pairs={{0,1},{1,0},{2,3},{3,2},{4,5},{5,4},{6,7},{7,6},{8,9},{9,8},{10,11... | collective-permute-start | bytes 1572872 | tf_op jit(solution)/shard_map/ppermute | solution.py:318
  358.0 29.6 %collective-permute-start.21 = (bf16[128,2048]{1,0:T(8,128)(2,1)}, bf16[128,2048]{1,0:T(8,128)(2,1)}, u32[]{:S(2)}, u32[]{:S(2)}) collective-permute-start(bf16[128,2048]{1,0:T(8,128)(2,1)} %slice.31.refs_7_), channel_id=1, source_target_pairs={{0,24},{4,28},{24,0},{28,4},{1,25},{5,29},{25,1},{29,5},{2,26},{6,... | collective-permute-start | bytes 1572872 | tf_op jit(solution)/shard_map/ppermute | solution.py:318
  373.2 14.4 %collective-permute-start.24 = (f32[2,256,128]{2,1,0:T(8,128)}, f32[2,256,128]{2,1,0:T(8,128)}, u32[]{:S(2)}, u32[]{:S(2)}) collective-permute-start(f32[2,256,128]{2,1,0:T(8,128)} %add.102.refs_8_), channel_id=1, source_target_pairs={{0,1},{1,0},{2,3},{3,2},{4,5},{5,4},{6,7},{7,6},{8,9},{9,8},{10,11... | collective-permute-start | bytes 786440 | tf_op jit(solution)/shard_map/ppermute | solution.py:318
  (14 other events, 342.8 us)

commit v3 on v2

--- a/solution.py
+++ b/solution.py
@@ -104,8 +104,14 @@
     quarter = columns // 4
     queries = quarter // R
     dense = any(factor is None for _, factor, _ in units)
+    jobs, seen = [], set()
+    for unit, (_, factor, _) in enumerate(units):
+        for place, which in enumerate(range(len(factors)) if factor is None else (factor,)):
+            jobs.append((unit, which, which not in seen, place == 0))
+            seen.add(which)
     first_total, own_total, partner_total, positions = totals if totals else (0, None, None, ())
     kinds = len(positions)
+    picks = 2
     held = len(sources) + len(factors) + len(after)
     added = [base for base in bases if base is not None]
 
@@ -113,7 +119,8 @@
         source_refs = refs[: len(sources)]
         factor_refs = refs[len(sources) : len(sources) + len(factors)]
         given = refs[held:]
-        token_buffer, factor_buffer, product_buffer, sum_buffer, token_done, factor_done = refs[-6:]
+        token_buffer, factor_buffer, product_buffer, sum_buffer, total_buffer = refs[-8:-3]
+        token_done, factor_done, total_done = refs[-3:]
         step = pl.program_id(0)
         first_core = flags_ref[0] == 0
         middle = flags_ref[1] == 1
@@ -128,6 +135,13 @@
                 origin.at[pl.ds(origin_row, length)],
                 token_buffer.at[unit, pl.ds(row, length)],
                 token_done.at[unit],
+            )
+
+        def total_copy(unit, kind):
+            return pltpu.make_async_copy(
+                given[kind].at[:, pl.ds((first_total + unit) * rows, rows)],
+                total_buffer.at[unit, kind],
+                total_done.at[unit, kind],
             )
 
         def fetch(unit):
@@ -161,7 +175,7 @@
                     keep_ref[side, span] = jnp.where(first_core, even, odd)
                     send_ref[side, span] = jnp.where(first_core, odd, even)
                 else:
-                    own, partner = given[0][side, span], given[1][side, span]
+                    own, partner = (total_buffer[unit, kind, side, span] for kind in range(2))
                     slots = pl.ds(unit * capacity + row // token_count, height // token_count)
                     for core, piece in enumerate((even, odd)):
                         total = jnp.where(first_core == (core == 0), own, partner)
@@ -173,23 +187,46 @@
                 token_buffer[unit, :height], factor_buffer[which], preferred_element_type=jnp.float32
             )
 
-        def compute(unit, fresh):
+        def wait_totals(unit):
+            if totals is not None:
+                for kind in range(2):
+                    total_copy(unit, kind).wait()
+
+        def issue(index):
+            if index < len(jobs):
+                unit, which, fresh, opens = jobs[index]
+                if opens:
+                    fetch(unit)
+                if fresh:
+                    factor_copy(which).start()
+                if opens and totals is not None:
+                    for kind in range(2):
+                        total_copy(unit, kind).start()
+
+        def compute(unit):
             _, factor, first = units[unit]
             height = part if factor is None else rows
-            token_copy(source_refs[0], 0, unit, 0, height).wait()
+            for index, (owner, which, fresh, opens) in enumerate(jobs):
+                if owner != unit:
+                    continue
+                if opens:
+                    token_copy(source_refs[0], 0, unit, 0, height).wait()
+                if fresh:
+                    factor_copy(which).wait()
+                issue(index + 2)
+                product = times(unit, height, which)
+                if factor is None:
+                    product_buffer[which] = product
+            wait_totals(unit)
             if factor is not None:
-                if factor in fresh:
-                    factor_copy(factor).wait()
-                give(unit, 0, rows, times(unit, rows, factor))
+                give(unit, 0, rows, product)
                 return
-            for which in range(len(factors)):
-                if which in fresh:
-                    factor_copy(which).wait()
-                product_buffer[which] = times(unit, part, which)
+            half = capacity // 2
             for entry in range(capacity):
                 which = order_ref[first, entry]
                 row = entry // 2 * token_count
-                product_buffer[len(factors) + entry // 8, entry % 8 * token_count : (entry % 8 + 1) * token_count] = (
+                target = entry % half * token_count
+                product_buffer[len(factors) + entry // half, target : target + token_count] = (
                     product_buffer[which, row : row + token_count]
                 )
             for half in range(2):
@@ -227,27 +264,24 @@
                     mine = parts[offset]
                     for index in range(1, 4):
                         mine = jnp.where(place == index, parts[index ^ offset], mine)
-                    if base_ref is not None:
-                        mine = mine + base_ref[offset]
-                    out_refs[kind][offset] = mine
+                    for pick in range(picks):
+                        piece = mine[:, pick * (mine.shape[1] // picks) : (pick + 1) * (mine.shape[1] // picks)]
+                        if base_ref is not None:
+                            piece = piece + base_ref[offset, pick]
+                        out_refs[kind][offset, pick] = piece
 
         @pl.when(step == 0)
         def _():
-            started = set()
-            for unit, (source, factor, first) in enumerate(units):
-                fetch(unit)
-                for which in range(len(factors)) if factor is None else (factor,):
-                    if which not in started:
-                        started.add(which)
-                        factor_copy(which).start()
-
-        seen = set()
-        for unit, (source, factor, first) in enumerate(units):
-            used = set(range(len(factors))) if factor is None else {factor}
-            pl.when(step == unit)(lambda unit=unit, fresh=used - seen: compute(unit, fresh))
-            seen |= used
+            issue(0)
+            issue(1)
+
+        for unit in range(count):
+            if totals is not None:
+                compute(unit)
+            else:
+                pl.when(step == unit)(lambda unit=unit: compute(unit))
         if totals is not None:
-            pl.when(step == count - 1)(finish)
+            finish()
 
     anywhere = pl.BlockSpec(memory_space=pltpu.HBM)
     scalars = pl.BlockSpec(memory_space=pltpu.SMEM)
@@ -262,15 +296,14 @@
         out_shape = (result, result)
         out_specs = (pl.BlockSpec((2, rows, quarter), lambda step: (0, step, 0)),) * 2
     else:
-        shape = (4, queries, positions[0].shape[1])
-        total_spec = pl.BlockSpec((2, rows, quarter), lambda step: (0, step + first_total, 0))
-        in_specs += [total_spec] * 2 + [whole(positions[0].shape)] * kinds + [whole(shape)] * len(added)
+        shape = (4, picks, queries, positions[0].shape[1] // picks)
+        in_specs += [anywhere] * 2 + [whole(positions[0].shape)] * kinds + [whole(shape)] * len(added)
         operands += [own_total, partner_total, *positions, *added]
         out_shape = (jax.ShapeDtypeStruct(shape, jnp.float32),) * kinds
         out_specs = (whole(shape),) * kinds
     return pl.pallas_call(
         body,
-        grid=(count,),
+        grid=(count if totals is None else 1,),
         out_shape=out_shape,
         in_specs=in_specs,
         out_specs=out_specs,
@@ -279,8 +312,10 @@
             pltpu.VMEM((len(factors), width, columns), factors[0].dtype),
             pltpu.VMEM((len(factors) + 2 if dense else 1, part, columns), jnp.float32),
             pltpu.VMEM((4, count * capacity, quarter), jnp.float32),
+            pltpu.VMEM((count if totals else 1, 2, 2, rows, quarter), jnp.float32),
             pltpu.SemaphoreType.DMA((count,)),
             pltpu.SemaphoreType.DMA((len(factors),)),
+            pltpu.SemaphoreType.DMA((count, 2)),
         ],
         compiler_params=pltpu.CompilerParams(vmem_limit_bytes=VMEM_BYTES),
     )(*operands)
@@ -304,7 +339,7 @@
     blocks, pick_count = candidates.shape
     entries = blocks * pick_count
     capacity = 2 * entries // 8
-    late = capacity // 2
+    late = 3 * blocks // 8
     early_rows = (blocks - late) * TOKENS_PER_BLOCK
     across_z = swap_pairs(8, 2)
     across_y = swap_pairs(8, 1)
@@ -358,11 +393,12 @@
     is_late = entry >= entries - 2 * late
     far_order, far_position = slots_of(jnp.where(is_late, 4, far_relative), pick_count, capacity)
     end_order = jnp.minimum(far_relative[entries - 2 * late :], 3)
-    order = jnp.concatenate([near_order, far_order, end_order[None]], axis=0)
+    end_order = end_order[None]
+    order = jnp.concatenate([near_order, far_order], axis=0)
     far_three = placed(far_position, 0, three, 0)
     far_fourth = placed(far_position, three, four, capacity - three)
     end_position = jnp.where(far_relative < 4, entry - (entries - 2 * late), -1)
-    end_position = placed(end_position, 0, capacity, 0)
+    end_position = placed(end_position, 0, 2 * late, 0)
 
     (near,) = grouped_products(
         first,
@@ -375,14 +411,14 @@
     )
     straight = [(1, 0, 4), (1, 1, 5), (1, 2, 6)]
     u_far = grouped_products(
-        straight, [grads, g_in, g_out], [u_factors, u_y, u_z], order, flags, after=(near, near_fourth, far_three, far_fourth, end_position)
+        straight, [grads, g_in, g_out], [u_factors, u_y, u_z], order, flags, after=(near, near_fourth, far_three, far_fourth, end_position, end_order)
     )
     g_far = summed(u_far)
     u_diagonal = grouped_products([(0, 0, 3), (1, 0, 7)], [grads, g_in, g_out], [u_d], order, flags, after=u_far[:1])
     g_diagonal = summed(u_diagonal)
-    ending = [(1, None, 8)]
+    ending = [(1, None, 0)]
     u_end = grouped_products(
-        ending, [grads, g_in, g_end], [u_factors, u_y, u_z, u_d], order, flags, after=u_diagonal[:1]
+        ending, [grads, g_in, g_end], [u_factors, u_y, u_z, u_d], end_order, flags, after=u_diagonal[:1]
     )
     g_ending = summed(u_end)
     (far,) = grouped_products(
@@ -408,7 +444,7 @@
         ending,
         [activations, a_in, a_end],
         [v_factors, v_y, v_z, v_d],
-        order,
+        end_order,
         flags,
         totals=(0, *g_ending, (end_position,)),
         bases=(far,),
@@ -418,7 +454,7 @@
     total = partial[0]
     for offset in (1, 2, 3):
         total = total + swap(partial[offset], swap_pairs(4, offset), "query")
-    return jnp.transpose(total.reshape(total.shape[0], pick_count, blocks), (2, 1, 0))
+    return jnp.transpose(total, (2, 0, 1))
 
 
 def solution(mesh):

time: 405 us -> 395 us (0.975)
  waiting for transfers between devices: 270 us -> 262 us
    ppermute x29, waiting for transfers between devices: 270 us -> 262 us  [swap(): return lax.ppermute(array, axis, pairs)]
  transfers between devices with their start and end apart: 29 -> 29, of which waited for: 10 -> 11; matrix products, arithmetic and copies ran while one was open for 7% -> 7% of each run, Pallas kernels for 12% -> 12%
where the time goes in v3:
time: 395 us; the launch traced here: 394 us
  waiting for transfers between devices  262 us (66%)
  Pallas kernels  64.1 us (16%)
  starting transfers between devices  37.9 us (10%)
  local copies, waits for them, and re-layouts  16.4 us (4%)
  other arithmetic  14 us (4%)
    ppermute x29, waiting for transfers between devices, swap(): return lax.ppermute(array, axis, pairs)  262 us
    pallas_call x8, Pallas kernels, grouped_products(): pl.pallas_call(body, grid=(count if totals is None else 1,), out_shape=ou...  64.1 us
    ppermute x29, starting transfers between devices, swap(): return lax.ppermute(array, axis, pairs)  37.9 us
  transfers between devices with their start and end apart: 29, of which 11 were waited for; matrix products, arithmetic and copies ran while one was open for 7% of the time, Pallas kernels for 12%

profile of v3, /device:TPU:9, one launch (start us, length us, event | category | flops | bytes accessed | tf_op | source)
XLA Modules:
  0.0 394.3 jit_solution(10960535485566275738)
XLA Ops:
  1.4 3.1 slice.28.refs_4_
  4.6 2.7 slice.29.refs_5_
  12.5 68.0 %collective-permute-done.2.refs_3_.refs_5_ = bf16[3584,512]{1,0:T(8,128)(2,1)} collective-permute-done((bf16[3584,512]{1,0:T(8,128)(2,1)}, bf16[3584,512]{1,0:T(8,128)(2,1)}, u32[]{:S(2)}, u32[]{:S(2)}) %collective-permute-start.2) | collective-permute-done | bytes 3670048 | tf_op jit(solution)/shard_map/ppermute | solution.py:353
  80.6 9.6 %shard_map.55 = (f32[2,768,128]{2,1,0:T(8,128)}, f32[2,768,128]{2,1,0:T(8,128)}) custom-call(s32[4,16]{1,0:T(4,128)} %reshape.104.order_ref, s32[3]{0:T(128)} %pad_add_fusion.1.flags_ref, bf16[512,3584]{1,0:T(8,128)(2,1)} %refs_0_.12, bf16[3584,512]{1,0:T(8,128)(2,1)} %refs_3_.5, bf16[3584,512]{1,0:T(8,128)(2,1)} %collective-permute-done.1.refs_2_.refs_4_, ...), custom_call_target="tpu_custom_call" | custom-call | tf_op jit(solution)/shard_map/pallas_call | solution.py:304
  91.8 4.6 %collective-permute-start.7 = (bf16[512,3584]{1,0:T(8,128)(2,1)}, bf16[512,3584]{1,0:T(8,128)(2,1)}, u32[]{:S(2)}, u32[]{:S(2)}) collective-permute-start(bf16[512,3584]{1,0:T(8,128)(2,1)} %refs_0_.12), channel_id=1, source_target_pairs={{8,16},{12,20},{16,8},{20,12},{9,17},{13,21},{17,9},{21,13},{10,18... | collective-permute-start | bytes 11010056 | tf_op jit(solution)/shard_map/ppermute | solution.py:353
  100.7 125.5 %collective-permute-done = s32[32,2]{1,0:T(8,128)S(1)} collective-permute-done((s32[32,2]{1,0:T(8,128)S(1)}, s32[32,2]{1,0:T(8,128)S(1)}, u32[]{:S(2)}, u32[]{:S(2)}) %collective-permute-start) | collective-permute-done | bytes 288 | tf_op jit(solution)/shard_map/ppermute | solution.py:353
  228.2 2.1 collective-permute-start.8
  236.1 36.7 %collective-permute-done.10.refs_2_.refs_4_ = bf16[2048,512]{1,0:T(8,128)(2,1)} collective-permute-done((bf16[2048,512]{1,0:T(8,128)(2,1)S(1)}, bf16[2048,512]{1,0:T(8,128)(2,1)}, u32[]{:S(2)}, u32[]{:S(2)}) %collective-permute-start.10) | collective-permute-done | bytes 2097184 | tf_op jit(solution)/shard_map/ppermute | solution.py:353
  272.8 1.8 collective-permute-start.17
  276.9 7.7 %shard_map.56.refs_6_.refs_8_ = f32[4,2,4,32]{3,2,1,0:T(4,128)} custom-call(s32[4,16]{1,0:T(4,128)} %reshape.104.order_ref, s32[3]{0:T(128)} %pad_add_fusion.1.flags_ref, bf16[512,2048]{1,0:T(8,128)(2,1)} %refs_0_.15, bf16[2048,512]{1,0:T(8,128)(2,1)} %refs_3_.7, bf16[2048,512]{1,0:T(8,128)(2,1)} %collective-permute-done.10.refs_2_.refs_4_, ...), custom_call_target="tpu_custom_call" | custom-call | tf_op jit(solution)/shard_map/pallas_call | solution.py:304
  284.6 9.9 %shard_map.57 = (f32[2,768,128]{2,1,0:T(8,128)}, f32[2,768,128]{2,1,0:T(8,128)}) custom-call(s32[8,16]{1,0:T(8,128)} %pad_add_fusion.order_ref, s32[3]{0:T(128)} %pad_add_fusion.1.flags_ref, bf16[512,3584]{1,0:T(8,128)(2,1)} %refs_0_.12, bf16[512,3584]{1,0:T(8,128)(2,1)} %collective-permute-done.7.refs_1_, bf16[320,3584]{1,0:T(8,128)(2,1)} %collective-permute-done.8.refs_2_, ...), custom_call_target="tpu_custom_call" | custom-call | tf_op jit(solution)/shard_map/pallas_call | solution.py:304
  296.1 3.1 collective-permute-start.3
  299.2 7.3 %shard_map.58 = (f32[2,512,128]{2,1,0:T(8,128)}, f32[2,512,128]{2,1,0:T(8,128)}) custom-call(s32[8,16]{1,0:T(8,128)} %pad_add_fusion.order_ref, s32[3]{0:T(128)} %pad_add_fusion.1.flags_ref, bf16[512,3584]{1,0:T(8,128)(2,1)} %refs_0_.12, bf16[512,3584]{1,0:T(8,128)(2,1)} %collective-permute-done.7.refs_1_, bf16[320,3584]{1,0:T(8,128)(2,1)} %collective-permute-done.8.refs_2_, ...), custom_call_target="tpu_custom_call" | custom-call | tf_op jit(solution)/shard_map/pallas_call | solution.py:304
  309.5 2.3 add.99
  313.0 8.5 %shard_map.59 = (f32[2,384,128]{2,1,0:T(8,128)}, f32[2,384,128]{2,1,0:T(8,128)}) custom-call(s32[1,24]{1,0:T(1,128)} %min.14.refs_11_.order_ref, s32[3]{0:T(128)} %pad_add_fusion.1.flags_ref, bf16[512,3584]{1,0:T(8,128)(2,1)} %refs_0_.12, bf16[512,3584]{1,0:T(8,128)(2,1)} %collective-permute-done.7.refs_1_, ...), custom_call_target="tpu_custom_call" | custom-call | tf_op jit(solution)/shard_map/pallas_call | solution.py:304
  325.2 5.5 %collective-permute-done.19 = f32[2,768,128]{2,1,0:T(8,128)} collective-permute-done((f32[2,768,128]{2,1,0:T(8,128)}, f32[2,768,128]{2,1,0:T(8,128)}, u32[]{:S(2)}, u32[]{:S(2)}) %collective-permute-start.19) | collective-permute-done | bytes 786464 | tf_op jit(solution)/shard_map/ppermute | solution.py:353
  334.4 2.6 collective-permute-start.20
  337.0 5.0 %collective-permute-done.15 = f32[2,512,128]{2,1,0:T(8,128)S(1)} collective-permute-done((f32[2,512,128]{2,1,0:T(8,128)S(1)}, f32[2,512,128]{2,1,0:T(8,128)S(1)}, u32[]{:S(2)}, u32[]{:S(2)}) %collective-permute-start.15) | collective-permute-done | bytes 524320 | tf_op jit(solution)/shard_map/ppermute | solution.py:353
  344.4 6.0 %collective-permute-done.23 = f32[2,384,128]{2,1,0:T(8,128)S(1)} collective-permute-done((f32[2,384,128]{2,1,0:T(8,128)S(1)}, f32[2,384,128]{2,1,0:T(8,128)S(1)}, u32[]{:S(2)}, u32[]{:S(2)}) %collective-permute-start.23) | collective-permute-done | bytes 393248 | tf_op jit(solution)/shard_map/ppermute | solution.py:353
  352.5 10.2 %collective-permute-done.3.refs_1_ = bf16[512,2048]{1,0:T(8,128)(2,1)} collective-permute-done((bf16[512,2048]{1,0:T(8,128)(2,1)}, bf16[512,2048]{1,0:T(8,128)(2,1)}, u32[]{:S(2)}, u32[]{:S(2)}) %collective-permute-start.3) | collective-permute-done | bytes 2097184 | tf_op jit(solution)/shard_map/ppermute | solution.py:353
  363.5 7.8 %shard_map.60.refs_9_ = f32[4,2,4,32]{3,2,1,0:T(4,128)} custom-call(s32[8,16]{1,0:T(8,128)} %pad_add_fusion.order_ref, s32[3]{0:T(128)} %pad_add_fusion.1.flags_ref, bf16[512,2048]{1,0:T(8,128)(2,1)} %refs_0_.15, bf16[512,2048]{1,0:T(8,128)(2,1)} %collective-permute-done.3.refs_1_, bf16[320,2048]{1,0:T(8,128)(2,1)} %collective-permute-done.4.refs_2_, ...), custom_call_target="tpu_custom_call" | custom-call | tf_op jit(solution)/shard_map/pallas_call | solution.py:304
  371.3 6.3 %shard_map.61 = (f32[4,2,4,32]{3,2,1,0:T(4,128)}, f32[4,2,4,32]{3,2,1,0:T(4,128)}) custom-call(s32[8,16]{1,0:T(8,128)} %pad_add_fusion.order_ref, s32[3]{0:T(128)} %pad_add_fusion.1.flags_ref, bf16[512,2048]{1,0:T(8,128)(2,1)} %refs_0_.15, bf16[512,2048]{1,0:T(8,128)(2,1)} %collective-permute-done.3.refs_1_, ...), custom_call_target="tpu_custom_call" | custom-call | tf_op jit(solution)/shard_map/pallas_call | solution.py:304
  377.7 7.1 %shard_map.62 = f32[4,2,4,32]{3,2,1,0:T(4,128)} custom-call(s32[1,24]{1,0:T(1,128)} %min.14.refs_11_.order_ref, s32[3]{0:T(128)} %pad_add_fusion.1.flags_ref, bf16[512,2048]{1,0:T(8,128)(2,1)} %refs_0_.15, bf16[512,2048]{1,0:T(8,128)(2,1)} %collective-permute-done.3.refs_1_, bf16[192,2048]{1,0:T(8,128)(2,1)} %collective-permute-done.21.refs_2_, ...), custom_call_target="tpu_custom_call" | custom-call | tf_op jit(solution)/shard_map/pallas_call | solution.py:304
  385.8 1.8 collective-permute-done.25
  (121 shorter events, 48.8 us)
Async XLA Ops:
  0.0 80.5 %collective-permute-start.2 = (bf16[3584,512]{1,0:T(8,128)(2,1)}, bf16[3584,512]{1,0:T(8,128)(2,1)}, u32[]{:S(2)}, u32[]{:S(2)}) collective-permute-start(bf16[3584,512]{1,0:T(8,128)(2,1)} %refs_3_.5), channel_id=1, source_target_pairs={{0,8},{4,12},{8,0},{12,4},{16,24},{20,28},{24,16},{28,20},{1,9},{5... | collective-permute-start | bytes 11010056 | tf_op jit(solution)/shard_map/ppermute | solution.py:353
  0.0 80.6 %collective-permute-start.1 = (bf16[3584,512]{1,0:T(8,128)(2,1)}, bf16[3584,512]{1,0:T(8,128)(2,1)}, u32[]{:S(2)}, u32[]{:S(2)}) collective-permute-start(bf16[3584,512]{1,0:T(8,128)(2,1)} %refs_3_.5), channel_id=1, source_target_pairs={{0,4},{4,0},{8,12},{12,8},{16,20},{20,16},{24,28},{28,24},{1,5},{5... | collective-permute-start | bytes 11010056 | tf_op jit(solution)/shard_map/ppermute | solution.py:353
  90.2 6.2 %collective-permute-start.11 = (f32[2,768,128]{2,1,0:T(8,128)}, f32[2,768,128]{2,1,0:T(8,128)S(1)}, u32[]{:S(2)}, u32[]{:S(2)}) collective-permute-start(f32[2,768,128]{2,1,0:T(8,128)} %get-tuple-element.18), channel_id=1, source_target_pairs={{0,1},{1,0},{2,3},{3,2},{4,5},{5,4},{6,7},{7,6},{8,9},{9,8},{10,11... | collective-permute-start | bytes 2359304 | tf_op jit(solution)/shard_map/ppermute | solution.py:353
  91.8 192.8 %collective-permute-start.7 = (bf16[512,3584]{1,0:T(8,128)(2,1)}, bf16[512,3584]{1,0:T(8,128)(2,1)}, u32[]{:S(2)}, u32[]{:S(2)}) collective-permute-start(bf16[512,3584]{1,0:T(8,128)(2,1)} %refs_0_.12), channel_id=1, source_target_pairs={{8,16},{12,20},{16,8},{20,12},{9,17},{13,21},{17,9},{21,13},{10,18... | collective-permute-start | bytes 11010056 | tf_op jit(solution)/shard_map/ppermute | solution.py:353
  97.7 129.5 %collective-permute-start.12 = (f32[2,768,128]{2,1,0:T(8,128)S(1)}, f32[2,768,128]{2,1,0:T(8,128)S(1)}, u32[]{:S(2)}, u32[]{:S(2)}) collective-permute-start(f32[2,768,128]{2,1,0:T(8,128)S(1)} %add.89), channel_id=1, source_target_pairs={{0,2},{1,3},{2,0},{3,1},{4,6},{5,7},{6,4},{7,5},{8,10},{9,11},{10,... | collective-permute-start | bytes 2359304 | tf_op jit(solution)/shard_map/ppermute | solution.py:353
  99.0 200.2 %collective-permute-start.9 = (bf16[3584,512]{1,0:T(8,128)(2,1)}, bf16[3584,512]{1,0:T(8,128)(2,1)}, u32[]{:S(2)}, u32[]{:S(2)}) collective-permute-start(bf16[3584,512]{1,0:T(8,128)(2,1)} %collective-permute-done.2.refs_3_.refs_5_), channel_id=1, source_target_pairs={{0,4},{4,0},{8,12},{12,8},{16,20},{20,16},{24,28},{28,24},{1,5},{5... | collective-permute-start | bytes 11010056 | tf_op jit(solution)/shard_map/ppermute | solution.py:353
  100.0 133.8 %collective-permute-start.5 = (bf16[2048,512]{1,0:T(8,128)(2,1)S(1)}, bf16[2048,512]{1,0:T(8,128)(2,1)}, u32[]{:S(2)}, u32[]{:S(2)}) collective-permute-start(bf16[2048,512]{1,0:T(8,128)(2,1)S(1)} %copy-done.1), channel_id=1, source_target_pairs={{0,8},{4,12},{8,0},{12,4},{16,24},{20,28},{24,16},{28,20},{1,9},{5... | collective-permute-start | bytes 6291464 | tf_op jit(solution)/shard_map/ppermute | solution.py:353
  100.0 126.1 %collective-permute-start = (s32[32,2]{1,0:T(8,128)S(1)}, s32[32,2]{1,0:T(8,128)S(1)}, u32[]{:S(2)}, u32[]{:S(2)}) collective-permute-start(s32[32,2]{1,0:T(8,128)S(1)} %copy-done.7), channel_id=1, source_target_pairs={{0,24},{4,28},{8,16},{12,20},{16,8},{20,12},{24,0},{28,4},{1,25},{... | collective-permute-start | bytes 776 | tf_op jit(solution)/shard_map/ppermute | solution.py:353
  226.1 46.7 %collective-permute-start.10 = (bf16[2048,512]{1,0:T(8,128)(2,1)S(1)}, bf16[2048,512]{1,0:T(8,128)(2,1)}, u32[]{:S(2)}, u32[]{:S(2)}) collective-permute-start(bf16[2048,512]{1,0:T(8,128)(2,1)S(1)} %copy-done.1), channel_id=1, source_target_pairs={{0,4},{4,0},{8,12},{12,8},{16,20},{20,16},{24,28},{28,24},{1,5},{5... | collective-permute-start | bytes 6291464 | tf_op jit(solution)/shard_map/ppermute | solution.py:353
  228.2 56.4 %collective-permute-start.8 = (bf16[320,3584]{1,0:T(8,128)(2,1)}, bf16[320,3584]{1,0:T(8,128)(2,1)}, u32[]{:S(2)}, u32[]{:S(2)}) collective-permute-start(bf16[320,3584]{1,0:T(8,128)(2,1)} %slice.28.refs_4_), channel_id=1, source_target_pairs={{0,24},{4,28},{24,0},{28,4},{1,25},{5,29},{25,1},{29,5},{2,26},{6,... | collective-permute-start | bytes 6881288 | tf_op jit(solution)/shard_map/ppermute | solution.py:353
  233.8 43.0 %collective-permute-start.13 = (f32[2,768,128]{2,1,0:T(8,128)S(1)}, f32[2,768,128]{2,1,0:T(8,128)}, u32[]{:S(2)}, u32[]{:S(2)}) collective-permute-start(f32[2,768,128]{2,1,0:T(8,128)S(1)} %add.90.refs_4_), channel_id=1, source_target_pairs={{0,1},{1,0},{2,3},{3,2},{4,5},{5,4},{6,7},{7,6},{8,9},{9,8},{10,11... | collective-permute-start | bytes 2359304 | tf_op jit(solution)/shard_map/ppermute | solution.py:353
  272.8 39.0 %collective-permute-start.17 = (bf16[192,3584]{1,0:T(8,128)(2,1)}, bf16[192,3584]{1,0:T(8,128)(2,1)}, u32[]{:S(2)}, u32[]{:S(2)}) collective-permute-start(bf16[192,3584]{1,0:T(8,128)(2,1)} %slice.29.refs_5_), channel_id=1, source_target_pairs={{0,24},{4,28},{24,0},{28,4},{1,25},{5,29},{25,1},{29,5},{2,26},{6,... | collective-permute-start | bytes 4128776 | tf_op jit(solution)/shard_map/ppermute | solution.py:353
  294.5 14.1 %collective-permute-start.18 = (f32[2,768,128]{2,1,0:T(8,128)}, f32[2,768,128]{2,1,0:T(8,128)}, u32[]{:S(2)}, u32[]{:S(2)}) collective-permute-start(f32[2,768,128]{2,1,0:T(8,128)} %get-tuple-element.23), channel_id=1, source_target_pairs={{0,1},{1,0},{2,3},{3,2},{4,5},{5,4},{6,7},{7,6},{8,9},{9,8},{10,11... | collective-permute-start | bytes 2359304 | tf_op jit(solution)/shard_map/ppermute | solution.py:353
  296.1 66.6 %collective-permute-start.3 = (bf16[512,2048]{1,0:T(8,128)(2,1)}, bf16[512,2048]{1,0:T(8,128)(2,1)}, u32[]{:S(2)}, u32[]{:S(2)}) collective-permute-start(bf16[512,2048]{1,0:T(8,128)(2,1)} %refs_0_.15), channel_id=1, source_target_pairs={{8,16},{12,20},{16,8},{20,12},{9,17},{13,21},{17,9},{21,13},{10,18... | collective-permute-start | bytes 6291464 | tf_op jit(solution)/shard_map/ppermute | solution.py:353
  306.5 15.0 %collective-permute-start.14 = (f32[2,512,128]{2,1,0:T(8,128)}, f32[2,512,128]{2,1,0:T(8,128)}, u32[]{:S(2)}, u32[]{:S(2)}) collective-permute-start(f32[2,512,128]{2,1,0:T(8,128)} %get-tuple-element.21), channel_id=1, source_target_pairs={{0,1},{1,0},{2,3},{3,2},{4,5},{5,4},{6,7},{7,6},{8,9},{9,8},{10,11... | collective-permute-start | bytes 1572872 | tf_op jit(solution)/shard_map/ppermute | solution.py:353
  306.9 26.6 %collective-permute-start.4 = (bf16[320,2048]{1,0:T(8,128)(2,1)}, bf16[320,2048]{1,0:T(8,128)(2,1)}, u32[]{:S(2)}, u32[]{:S(2)}) collective-permute-start(bf16[320,2048]{1,0:T(8,128)(2,1)} %slice.30.refs_6_), channel_id=1, source_target_pairs={{0,24},{4,28},{24,0},{28,4},{1,25},{5,29},{25,1},{29,5},{2,26},{6,... | collective-permute-start | bytes 3932168 | tf_op jit(solution)/shard_map/ppermute | solution.py:353
  308.6 62.7 %collective-permute-start.6 = (bf16[2048,512]{1,0:T(8,128)(2,1)}, bf16[2048,512]{1,0:T(8,128)(2,1)}, u32[]{:S(2)}, u32[]{:S(2)}) collective-permute-start(bf16[2048,512]{1,0:T(8,128)(2,1)} %collective-permute-done.5.refs_3_.refs_5_), channel_id=1, source_target_pairs={{0,4},{4,0},{8,12},{12,8},{16,20},{20,16},{24,28},{28,24},{1,5},{5... | collective-permute-start | bytes 6291464 | tf_op jit(solution)/shard_map/ppermute | solution.py:353
  311.8 18.9 %collective-permute-start.19 = (f32[2,768,128]{2,1,0:T(8,128)}, f32[2,768,128]{2,1,0:T(8,128)}, u32[]{:S(2)}, u32[]{:S(2)}) collective-permute-start(f32[2,768,128]{2,1,0:T(8,128)} %add.99), channel_id=1, source_target_pairs={{0,2},{1,3},{2,0},{3,1},{4,6},{5,7},{6,4},{7,5},{8,10},{9,11},{10,... | collective-permute-start | bytes 2359304 | tf_op jit(solution)/shard_map/ppermute | solution.py:353
  323.9 18.1 %collective-permute-start.15 = (f32[2,512,128]{2,1,0:T(8,128)S(1)}, f32[2,512,128]{2,1,0:T(8,128)S(1)}, u32[]{:S(2)}, u32[]{:S(2)}) collective-permute-start(f32[2,512,128]{2,1,0:T(8,128)S(1)} %add.97), channel_id=1, source_target_pairs={{0,2},{1,3},{2,0},{3,1},{4,6},{5,7},{6,4},{7,5},{8,10},{9,11},{10,... | collective-permute-start | bytes 1572872 | tf_op jit(solution)/shard_map/ppermute | solution.py:353
  330.8 19.7 %collective-permute-start.23 = (f32[2,384,128]{2,1,0:T(8,128)S(1)}, f32[2,384,128]{2,1,0:T(8,128)S(1)}, u32[]{:S(2)}, u32[]{:S(2)}) collective-permute-start(f32[2,384,128]{2,1,0:T(8,128)S(1)} %add.101), channel_id=1, source_target_pairs={{0,2},{1,3},{2,0},{3,1},{4,6},{5,7},{6,4},{7,5},{8,10},{9,11},{10,... | collective-permute-start | bytes 1179656 | tf_op jit(solution)/shard_map/ppermute | solution.py:353
  334.4 29.1 %collective-permute-start.20 = (f32[2,768,128]{2,1,0:T(8,128)S(1)}, f32[2,768,128]{2,1,0:T(8,128)}, u32[]{:S(2)}, u32[]{:S(2)}) collective-permute-start(f32[2,768,128]{2,1,0:T(8,128)S(1)} %add.100.refs_7_), channel_id=1, source_target_pairs={{0,1},{1,0},{2,3},{3,2},{4,5},{5,4},{6,7},{7,6},{8,9},{9,8},{10,11... | collective-permute-start | bytes 2359304 | tf_op jit(solution)/shard_map/ppermute | solution.py:353
  342.0 35.7 %collective-permute-start.21 = (bf16[192,2048]{1,0:T(8,128)(2,1)}, bf16[192,2048]{1,0:T(8,128)(2,1)}, u32[]{:S(2)}, u32[]{:S(2)}) collective-permute-start(bf16[192,2048]{1,0:T(8,128)(2,1)} %slice.31.refs_7_), channel_id=1, source_target_pairs={{0,24},{4,28},{24,0},{28,4},{1,25},{5,29},{25,1},{29,5},{2,26},{6,... | collective-permute-start | bytes 2359304 | tf_op jit(solution)/shard_map/ppermute | solution.py:353
  350.4 20.9 %collective-permute-start.16 = (f32[2,512,128]{2,1,0:T(8,128)}, f32[2,512,128]{2,1,0:T(8,128)}, u32[]{:S(2)}, u32[]{:S(2)}) collective-permute-start(f32[2,512,128]{2,1,0:T(8,128)} %add.98.refs_4_), channel_id=1, source_target_pairs={{0,1},{1,0},{2,3},{3,2},{4,5},{5,4},{6,7},{7,6},{8,9},{9,8},{10,11... | collective-permute-start | bytes 1572872 | tf_op jit(solution)/shard_map/ppermute | solution.py:353
  362.6 15.0 %collective-permute-start.24 = (f32[2,384,128]{2,1,0:T(8,128)}, f32[2,384,128]{2,1,0:T(8,128)}, u32[]{:S(2)}, u32[]{:S(2)}) collective-permute-start(f32[2,384,128]{2,1,0:T(8,128)} %add.102.refs_8_), channel_id=1, source_target_pairs={{0,1},{1,0},{2,3},{3,2},{4,5},{5,4},{6,7},{7,6},{8,9},{9,8},{10,11... | collective-permute-start | bytes 1179656 | tf_op jit(solution)/shard_map/ppermute | solution.py:353
  (19 other events, 708.6 us)
